TPU v7x, 32 devices: a whole 2x2x4 slice. The times are simulated.
32 devices in a mesh: group: 2 (over x), ingroup: 4 (over y, core), hid: 4 (over z).
Axes of the slice: x: 2, y: 2, z: 4, core: 2. Of those that a mesh axis runs over, the one named last changes fastest.
Arguments:
- tokens: bfloat16 [128, 2048], P(('group', 'hid')), may hold values from -6 to 6
- grad_mixed: bfloat16 [128, 2048], P(('group', 'hid')), may hold values from -6 to 6
- expert_ids: int32 [128, 6], P(('group', 'hid')), may hold values from 0 to 63, all different within a row; in each aligned block of 16 rows (0 to 15, 16 to 31, ...) at most 2 rows name the same one
- gate_weight: float32 [128, 6], P(('group', 'hid')), may hold values from 0.05 to 1
- w_gate: bfloat16 [64, 2048, 1408], P('hid', None, 'ingroup'), may hold values from -0.125 to 0.125
- w_up: bfloat16 [64, 2048, 1408], P('hid', None, 'ingroup'), may hold values from -0.125 to 0.125
- w_down: bfloat16 [64, 1408, 2048], P('hid', 'ingroup'), may hold values from -0.15625 to 0.15625
Outputs:
- mixed: bfloat16 [128, 2048], P(('group', 'hid'), 'ingroup')
- grad_tokens: bfloat16 [128, 2048], P(('group', 'hid'), 'ingroup')
- grad_gate: float32 [64, 2048, 1408], P('hid', 'group', 'ingroup')
- grad_up: float32 [64, 2048, 1408], P('hid', 'group', 'ingroup')
- grad_down: float32 [64, 1408, 2048], P('hid', 'ingroup', 'group')
Inputs may be any that keep to these rules, and one draw needn't show every extreme that they name: `expert_ids`: each row names 6 different experts. Among the 16 tokens of one index of group and hid (aligned blocks of rows), no expert is named more than 2 times, and that bound is reached.
All inputs are finite; a program needn't handle non-finite values.
Results may differ from a plain program's by a relative error of at most 0.015.
Values may be sent and summed in bfloat16 or wider, within the bound.
No kernel may reach another device: no remote copies, remote signals or barrier semaphores. Data moves between devices by JAX's collectives and lax.ppermute only.
A program may use at most 256 MiB of HBM per device.

v0:
```python
import jax
import jax.numpy as jnp
from jax import lax
from jax.sharding import PartitionSpec as P

TOP = 6


def shards(tokens, grad_mixed, expert_ids, gate_weight, w_gate, w_up, w_down):
    tok_count = tokens.shape[0]
    width = tokens.shape[1]
    n_hid = lax.axis_size("hid")
    exp_dev = w_gate.shape[0]
    experts_all = exp_dev * n_hid
    capacity = tok_count // 8
    slots_total = experts_all * capacity
    flat = expert_ids.reshape(tok_count * TOP)
    onehot = (flat[:, None] == jnp.arange(experts_all, dtype=jnp.int32)[None, :]).astype(jnp.int32)
    rank = jnp.sum((jnp.cumsum(onehot, axis=0) - onehot) * onehot, axis=1)
    owner_idx = flat // exp_dev
    local_idx = flat % exp_dev
    slot = (local_idx * n_hid + owner_idx) * capacity + rank
    token_index = jnp.arange(tok_count * TOP, dtype=jnp.int32) // TOP
    token_of = jnp.zeros((slots_total,), jnp.int32).at[slot].set(token_index)
    live_of = jnp.zeros((slots_total,), jnp.bool_).at[slot].set(True)
    gate_of = (
        jnp.zeros((slots_total,), jnp.float32).at[slot].set(gate_weight.reshape(tok_count * TOP))
    )
    send_x = jnp.where(live_of[:, None], tokens[token_of], jnp.zeros((), jnp.bfloat16))
    send_g = (gate_of[:, None] * grad_mixed[token_of].astype(jnp.float32)).astype(jnp.bfloat16)
    shape_whole = (exp_dev, n_hid, capacity, width)
    recv_x, recv_g = (
        lax.all_to_all(send_x.reshape(shape_whole), "hid", split_axis=1, concat_axis=1, tiled=True),
        lax.all_to_all(send_g.reshape(shape_whole), "hid", split_axis=1, concat_axis=1, tiled=True),
    )
    rows = n_hid * capacity
    x_rows = recv_x.reshape(exp_dev, rows, width)
    gated = recv_g.reshape(exp_dev, rows, width)
    gate_pre = jnp.einsum("emd,edh->emh", x_rows, w_gate, preferred_element_type=jnp.float32)
    up_pre = jnp.einsum("emd,edh->emh", x_rows, w_up, preferred_element_type=jnp.float32)
    sigmoid_gate = jax.nn.sigmoid(gate_pre)
    silu = gate_pre * sigmoid_gate
    hidden = (silu * up_pre).astype(jnp.bfloat16)
    out_part = jnp.einsum("emh,ehd->emd", hidden, w_down, preferred_element_type=jnp.float32)
    d_hidden = jnp.einsum("emd,ehd->emh", gated, w_down, preferred_element_type=jnp.float32)
    d_up = (d_hidden * silu).astype(jnp.bfloat16)
    d_gate = (d_hidden * up_pre * sigmoid_gate * (1.0 + gate_pre * (1.0 - sigmoid_gate))).astype(
        jnp.bfloat16
    )
    term_down = jnp.einsum("emh,emd->ehd", hidden, gated, preferred_element_type=jnp.float32)
    term_gate = jnp.einsum("emd,emh->edh", x_rows, d_gate, preferred_element_type=jnp.float32)
    term_up = jnp.einsum("emd,emh->edh", x_rows, d_up, preferred_element_type=jnp.float32)
    in_part = jnp.einsum("emh,edh->emd", d_gate, w_gate, preferred_element_type=jnp.float32)
    in_part = in_part + jnp.einsum("emh,edh->emd", d_up, w_up, preferred_element_type=jnp.float32)
    grad_gate, grad_up, grad_down = (
        lax.psum_scatter(
            term_gate.astype(jnp.bfloat16), "group", scatter_dimension=1, tiled=True
        ).astype(jnp.float32),
        lax.psum_scatter(
            term_up.astype(jnp.bfloat16), "group", scatter_dimension=1, tiled=True
        ).astype(jnp.float32),
        lax.psum_scatter(
            term_down.astype(jnp.bfloat16), "group", scatter_dimension=2, tiled=True
        ).astype(jnp.float32),
    )
    out_share, in_share = (
        lax.psum_scatter(
            out_part.astype(jnp.bfloat16), "ingroup", scatter_dimension=2, tiled=True
        ).astype(jnp.float32),
        lax.psum_scatter(
            in_part.astype(jnp.bfloat16), "ingroup", scatter_dimension=2, tiled=True
        ).astype(jnp.float32),
    )
    narrow = out_share.shape[2]
    out_share = out_share.astype(jnp.bfloat16)
    in_share = in_share.astype(jnp.bfloat16)
    back_shape = (exp_dev, n_hid, capacity, narrow)
    home_out, home_in = (
        lax.all_to_all(
            out_share.reshape(back_shape), "hid", split_axis=1, concat_axis=1, tiled=True
        ),
        lax.all_to_all(
            in_share.reshape(back_shape), "hid", split_axis=1, concat_axis=1, tiled=True
        ),
    )
    picked_out = home_out.reshape(slots_total, narrow)[slot].reshape(tok_count, TOP, narrow)
    picked_in = home_in.reshape(slots_total, narrow)[slot].reshape(tok_count, TOP, narrow)
    mixed = jnp.sum(gate_weight[:, :, None] * picked_out.astype(jnp.float32), axis=1).astype(
        jnp.bfloat16
    )
    grad_tokens = jnp.sum(picked_in.astype(jnp.float32), axis=1).astype(jnp.bfloat16)
    return (mixed, grad_tokens, grad_gate, grad_up, grad_down)


def solution(mesh):
    placed = (
        P(("group", "hid"), None),
        P(("group", "hid"), None),
        P(("group", "hid"), None),
        P(("group", "hid"), None),
        P("hid", None, "ingroup"),
        P("hid", None, "ingroup"),
        P("hid", "ingroup", None),
    )
    return jax.shard_map(
        shards,
        mesh=mesh,
        in_specs=placed,
        out_specs=(
            P(("group", "hid"), "ingroup"),
            P(("group", "hid"), "ingroup"),
            P("hid", "group", "ingroup"),
            P("hid", "group", "ingroup"),
            P("hid", "ingroup", "group"),
        ),
        check_vma=False,
    )
```

profile of v0, /device:TPU:0, one launch (start us, length us, event | category | flops | bytes accessed | tf_op | source)
XLA Modules:
  0.0 928.8 jit_solution(1965958051563612181)
XLA Ops:
  11.9 1.3 broadcast_select_fusion
  13.2 6.3 all-to-all-start
  21.6 2.3 gather_fusion.2
  26.5 7.6 all-to-all-done
  34.1 3.5 all-to-all-start.2
  38.5 10.6 %fusion.14 = f32[16,8,352]{2,1,0:T(8,128)S(1)} fusion(bf16[16,8,2048]{2,1,0:T(8,128)(2,1)S(1)} %reshape.181, bf16[16,2048,352]{1,2,0:T(8,128)(2,1)} %param.12), kind=kOutput, calls=%fused_computation.49 | convolution fusion | flops 184549376 | bytes 23773184 | tf_op jit(solution)/shard_map/emd,edh->emh/dot_general | solution.py:40
  49.1 10.6 %fusion.13 = f32[16,8,352]{2,1,0:T(8,128)S(1)} fusion(bf16[16,8,2048]{2,1,0:T(8,128)(2,1)S(1)} %reshape.181, bf16[16,2048,352]{1,2,0:T(8,128)(2,1)} %param.11), kind=kOutput, calls=%fused_computation.48 | convolution fusion | flops 184549376 | bytes 23773184 | tf_op jit(solution)/shard_map/emd,edh->emh/dot_general | solution.py:39
  60.5 10.8 %multiply_convert_fusion = (bf16[16,8,352]{2,1,0:T(8,128)(2,1)S(1)}, bf16[16,8,352]{2,1,0:T(8,128)(2,1)S(1)}, bf16[16,8,352]{2,1,0:T(8,128)(2,1)S(1)}) fusion(f32[16,8,352]{2,1,0:T(8,128)S(1)} %fusion.13, f32[16,8,352]{2,1,0:T(8,128)S(1)} %fusion.14, bf16[16,8,2048]{2,1,0:T(8,128)(2,1)S(1)} %reshape.185, bf16[16,352,2048]{2,1,0:T(8,128)(2,1)} %param.13), kind=kOutput, calls=%fused_computation.17 | convolution fusion | flops 185225216 | bytes 24223744 | tf_op jit(solution)/shard_map/emd,ehd->emh/dot_general | solution.py:45
  71.3 11.4 %convolution_convert_fusion.3 = bf16[16,8,2048]{2,1,0:T(8,128)(2,1)} fusion(bf16[16,8,352]{2,1,0:T(8,128)(2,1)S(1)} %get-tuple-element.7, bf16[16,352,2048]{2,1,0:T(8,128)(2,1)} %param.13), kind=kOutput, calls=%fused_computation.12 | convolution fusion | flops 184811520 | bytes 23683072 | tf_op jit(solution)/shard_map/emh,ehd->emd/dot_general | solution.py:44
  83.0 9.3 fusion.15
  92.3 11.5 %fusion = bf16[16,8,2048]{2,1,0:T(8,128)(2,1)} fusion(f32[16,8,2048]{2,1,0:T(8,128)S(1)} %fusion.15, bf16[16,8,352]{2,1,0:T(8,128)(2,1)S(1)} %get-tuple-element.5, bf16[16,2048,352]{1,2,0:T(8,128)(2,1)} %param.12), kind=kOutput, calls=%fused_computation.11 | convolution fusion | flops 185073664 | bytes 24731648 | tf_op jit(solution)/shard_map/emh,edh->emd/dot_general | solution.py:54
  103.8 11.4 %convolution_convert_fusion = bf16[16,352,2048]{2,1,0:T(8,128)(2,1)} fusion(bf16[16,8,352]{2,1,0:T(8,128)(2,1)S(1)} %get-tuple-element.7, bf16[16,8,2048]{2,1,0:T(8,128)(2,1)S(1)} %reshape.185), kind=kOutput, calls=%fused_computation.7 | convolution fusion | flops 196083712 | bytes 23683072 | tf_op jit(solution)/shard_map/emh,emd->ehd/dot_general | solution.py:50
  115.3 11.4 %convolution_convert_fusion.1 = bf16[16,2048,352]{1,2,0:T(8,128)(2,1)} fusion(bf16[16,8,2048]{2,1,0:T(8,128)(2,1)S(1)} %reshape.181, bf16[16,8,352]{2,1,0:T(8,128)(2,1)S(1)} %get-tuple-element.5), kind=kOutput, calls=%fused_computation.8 | convolution fusion | flops 196083712 | bytes 23683072 | tf_op jit(solution)/shard_map/emd,emh->edh/dot_general | solution.py:52
  127.1 11.4 %convolution_convert_fusion.2 = bf16[16,2048,352]{1,2,0:T(8,128)(2,1)} fusion(bf16[16,8,2048]{2,1,0:T(8,128)(2,1)S(1)} %reshape.181, bf16[16,8,352]{2,1,0:T(8,128)(2,1)S(1)} %get-tuple-element.6), kind=kOutput, calls=%fused_computation.9 | convolution fusion | flops 196083712 | bytes 23683072 | tf_op jit(solution)/shard_map/emd,emh->edh/dot_general | solution.py:51
  140.4 4.8 all-to-all-start.1
  146.9 4.2 all-to-all-done.1
  151.1 3.3 all-to-all-start.3
  155.4 4.9 all-to-all-done.3
  162.8 227.0 %reduce-scatter.14.cloned.1.call-done = bf16[16,352,1024]{2,1,0:T(8,128)(2,1)} async-done(((bf16[16,352,2048]{2,1,0:T(8,128)(2,1)}), bf16[16,352,1024]{2,1,0:T(8,128)(2,1)}) %reduce-scatter.14.cloned.1.call-update) | async-done | bytes 11534352 | tf_op jit(solution)/shard_map/reduce_scatter | solution.py:62
  389.7 13.4 %convert_element_type.79 = f32[16,352,1024]{2,1,0:T(8,128)} convert(bf16[16,352,1024]{2,1,0:T(8,128)(2,1)} %reduce-scatter.14.cloned.1.call-done) | non-fusion elementwise | flops 5767168 | bytes 34603008 | tf_op jit(solution)/shard_map/convert_element_type | solution.py:64
  403.2 246.2 %reduce-scatter.12.cloned.1.call-done = bf16[16,1024,352]{1,2,0:T(8,128)(2,1)} async-done(((bf16[16,2048,352]{1,2,0:T(8,128)(2,1)}), bf16[16,1024,352]{1,2,0:T(8,128)(2,1)}) %reduce-scatter.12.cloned.1.call-update) | async-done | bytes 11534352 | tf_op jit(solution)/shard_map/reduce_scatter | solution.py:59
  649.3 13.5 %convert_element_type.77 = f32[16,1024,352]{1,2,0:T(8,128)} convert(bf16[16,1024,352]{1,2,0:T(8,128)(2,1)} %reduce-scatter.12.cloned.1.call-done) | non-fusion elementwise | flops 5767168 | bytes 34603008 | tf_op jit(solution)/shard_map/convert_element_type | solution.py:61
  662.8 246.1 %reduce-scatter.10.cloned.1.call-done = bf16[16,1024,352]{1,2,0:T(8,128)(2,1)} async-done(((bf16[16,2048,352]{1,2,0:T(8,128)(2,1)}), bf16[16,1024,352]{1,2,0:T(8,128)(2,1)}) %reduce-scatter.10.cloned.1.call-update) | async-done | bytes 11534352 | tf_op jit(solution)/shard_map/reduce_scatter | solution.py:56
  908.9 13.3 %convert_element_type.75 = f32[16,1024,352]{1,2,0:T(8,128)} convert(bf16[16,1024,352]{1,2,0:T(8,128)(2,1)} %reduce-scatter.10.cloned.1.call-done) | non-fusion elementwise | flops 5767168 | bytes 34603008 | tf_op jit(solution)/shard_map/convert_element_type | solution.py:58
  (61 shorter events, 18.4 us)
Async XLA Ops:
  7.2 3.4 copy-start
  13.2 20.8 %all-to-all-start = ((bf16[16,4,2,2048]{3,2,0,1:T(2,128)(2,1)}), bf16[16,4,2,2048]{3,2,0,1:T(2,128)(2,1)S(1)}, u32[]{:S(2)}, u32[]{:S(2)}) async-start(bf16[16,4,2,2048]{3,2,0,1:T(2,128)(2,1)} %broadcast_select_fusion), calls=%async_computation | async-start | bytes 1048576 | tf_op jit(solution)/shard_map/all_to_all | solution.py:33
  34.1 25.7 %all-to-all-start.2 = ((bf16[16,4,2,2048]{3,2,0,1:T(2,128)(2,1)}), bf16[16,4,2,2048]{3,2,0,1:T(2,128)(2,1)S(1)}, u32[]{:S(2)}, u32[]{:S(2)}) async-start(bf16[16,4,2,2048]{3,2,0,1:T(2,128)(2,1)} %copy.59), calls=%async_computation.3 | async-start | bytes 1048576 | tf_op jit(solution)/shard_map/all_to_all | solution.py:34
  37.5 101.1 %reduce-scatter.6.cloned.1.call-start = ((), (), s32[]{:S(2)}) async-start(), calls=%async_computation.9 | async-start | bytes 655360 | tf_op jit(solution)/shard_map/reduce_scatter | solution.py:67
  82.7 62.5 %reduce-scatter.8.cloned.1.call-start = ((), (), s32[]{:S(2)}) async-start(), calls=%async_computation.10 | async-start | bytes 655360 | tf_op jit(solution)/shard_map/reduce_scatter | solution.py:70
  103.8 285.9 %reduce-scatter.14.cloned.1.call-start = ((), (), s32[]{:S(2)}) async-start(), calls=%async_computation.13 | async-start | bytes 34603008 | tf_op jit(solution)/shard_map/reduce_scatter | solution.py:62
  115.3 534.0 %reduce-scatter.12.cloned.1.call-start = ((), (), s32[]{:S(2)}) async-start(), calls=%async_computation.12 | async-start | bytes 34603008 | tf_op jit(solution)/shard_map/reduce_scatter | solution.py:59
  126.8 782.1 %reduce-scatter.10.cloned.1.call-start = ((), (), s32[]{:S(2)}) async-start(), calls=%async_computation.11 | async-start | bytes 34603008 | tf_op jit(solution)/shard_map/reduce_scatter | solution.py:56
  140.4 10.8 %all-to-all-start.1 = ((bf16[16,4,2,512]{3,2,0,1:T(2,128)(2,1)}), bf16[16,4,2,512]{3,2,0,1:T(2,128)(2,1)S(1)}, u32[]{:S(2)}, u32[]{:S(2)}) async-start(bf16[16,4,2,512]{3,2,0,1:T(2,128)(2,1)} %copy.54), calls=%async_computation.2 | async-start | bytes 262144 | tf_op jit(solution)/shard_map/all_to_all | solution.py:79
  151.1 9.2 all-to-all-start.3
  649.3 272.9 %copy-start.1 = (bf16[16,2048]{1,0:T(8,128)(2,1)S(1)}, bf16[16,2048]{1,0:T(8,128)(2,1)}, u32[]{:S(2)}) copy-start(bf16[16,2048]{1,0:T(8,128)(2,1)} %param.7) | copy-start | bytes 196612
Sparse Core Ops, SparseCore 0:
  82.9 22.8 reduce-scatter.5
  108.3 21.6 reduce-scatter.7
  132.9 256.8 reduce-scatter.13
  392.5 256.8 reduce-scatter.11
  652.0 256.8 reduce-scatter.9
where the time goes:
time: 930 us; the launch traced here: 929 us
  waiting for transfers between devices  736 us (79%)
  matrix products  98.6 us (11%)
  other arithmetic  44 us (5%)
  starting transfers between devices  18.8 us (2%)
  local copies, waits for them, and re-layouts  17.2 us (2%)
  between operations  14 us (2%)
    reduce_scatter x1, waiting for transfers between devices, shards(): lax.psum_scatter(term_up.astype(jnp.bfloat16), 'group', scatter_dimension...  246 us
    reduce_scatter x1, waiting for transfers between devices, shards(): lax.psum_scatter(term_gate.astype(jnp.bfloat16), 'group', scatter_dimensi...  246 us
    reduce_scatter x1, waiting for transfers between devices, shards(): lax.psum_scatter(term_down.astype(jnp.bfloat16), 'group', scatter_dimensi...  227 us
    convert_element_type x3, other arithmetic, shards(): grad_gate, grad_up, grad_down = (lax.psum_scatter(term_gate.astype(jnp.bf...  40.2 us
  transfers between devices with their start and end apart: 9, of which 6 were waited for; matrix products, arithmetic and copies ran while one was open for 13% of the time, Pallas kernels for 0%

commit v1 on v0

--- a/solution.py
+++ b/solution.py
@@ -1,12 +1,16 @@
+import functools
+
 import jax
 import jax.numpy as jnp
 from jax import lax
+from jax.experimental import pallas as pl
+from jax.experimental.pallas import tpu as pltpu
 from jax.sharding import PartitionSpec as P
 
 TOP = 6
 
 
-def shards(tokens, grad_mixed, expert_ids, gate_weight, w_gate, w_up, w_down):
+def plain(tokens, grad_mixed, expert_ids, gate_weight, w_gate, w_up, w_down):
     tok_count = tokens.shape[0]
     width = tokens.shape[1]
     n_hid = lax.axis_size("hid")
@@ -92,6 +96,239 @@
     return (mixed, grad_tokens, grad_gate, grad_up, grad_down)
 
 
+def middle_kernel(sizes, scal, u_ref, v_ref, wg_ref, wu_ref, wd_ref,
+                  part_ref, act_ref, xs_ref, gs_ref,
+                  x_scr, g_scr, c_scr, ct_scr, wbuf, acc_o, acc_i, act_scr, sem):
+    n_group, n_ingroup, n_hid, tok, experts, half, cap = sizes
+    ff, width = wbuf.shape[2], wbuf.shape[3]
+    exp_own = wbuf.shape[1]
+    rows = n_group * n_hid * tok
+    wide = width // 2
+    g, i, h = scal[0], scal[1], scal[2]
+    core = lax.rem(i, 2)
+    base = g * exp_own
+
+    def fetch(e, k, ref):
+        return pltpu.make_async_copy(ref.at[base + e], wbuf.at[k, e], sem.at[k, e])
+
+    for e in range(exp_own):
+        for k, ref in enumerate((wg_ref, wu_ref, wd_ref)):
+            fetch(e, k, ref).start()
+
+    for ref, part in ((u_ref, core), (v_ref, 1 - core)):
+        for s in range(n_group):
+            for d in range(n_hid):
+                block = lax.rem(g + s, n_group) * n_hid + lax.rem(h - d + n_hid, n_hid)
+                at = pl.ds(pl.multiple_of(block * tok, tok), tok)
+                msg = s * n_hid + d
+                x_scr[part, at, :] = ref[msg, :, :wide]
+                g_scr[part, at, :] = ref[msg, :, wide:2 * wide]
+                c_scr[part, at, :] = ref[msg, :, 2 * wide:].astype(jnp.float32)
+
+    lanes = c_scr.shape[2]
+    first, second = c_scr[0], c_scr[1]
+    weight = first + pltpu.roll(first, lanes - experts, 1) + second
+    lane = lax.broadcasted_iota(jnp.int32, (rows, lanes), 1)
+    weight = jnp.where(lane < experts, weight, 0.0)
+    routed = (weight > 0).astype(jnp.bfloat16)
+    row_a = lax.broadcasted_iota(jnp.int32, (rows, rows), 0)
+    row_b = lax.broadcasted_iota(jnp.int32, (rows, rows), 1)
+    before = ((row_a // tok == row_b // tok) & (row_b < row_a)).astype(jnp.bfloat16)
+    rank = jnp.dot(before, routed, preferred_element_type=jnp.float32)
+    block_of = (lax.broadcasted_iota(jnp.int32, (rows, lanes), 0) // tok).astype(jnp.float32)
+    slot = jnp.where(weight > 0, rank + cap * block_of, -1.0)
+    ct_scr[...] = weight.T
+    slots = n_group * n_hid * cap
+    spread_e = lax.broadcasted_iota(jnp.int32, (lanes, exp_own * slots), 0)
+    spread_l = lax.broadcasted_iota(jnp.int32, (lanes, exp_own * slots), 1)
+    lane_s = lax.broadcasted_iota(jnp.int32, (rows, exp_own * slots), 1)
+    picks = []
+    for which in range(n_group):
+        owner = h * (exp_own * n_group) + lax.rem(g + which, n_group) * exp_own
+        spread = (spread_e == owner + spread_l // slots).astype(jnp.bfloat16)
+        slot_l = jnp.dot(slot.astype(jnp.bfloat16), spread, preferred_element_type=jnp.float32)
+        pick = (slot_l == (lane_s % slots).astype(jnp.float32)).astype(jnp.float32)
+        pick_t = pick.T.astype(jnp.bfloat16)
+        picks.append(pick.astype(jnp.bfloat16))
+        xs_ref[which] = jnp.dot(pick_t, x_scr[g], preferred_element_type=jnp.float32).astype(jnp.bfloat16)
+        gs_ref[which] = jnp.dot(pick_t, g_scr[g], preferred_element_type=jnp.float32).astype(jnp.bfloat16)
+
+    acc_o[...] = jnp.zeros_like(acc_o)
+    acc_i[...] = jnp.zeros_like(acc_i)
+    act_scr[...] = jnp.zeros_like(act_scr)
+    pair = 2
+    nt = (((1,), (1,)), ((), ()))
+    tn = (((0,), (0,)), ((), ()))
+
+    def both(k, e0, tok_scr):
+        w = wbuf[k, pl.ds(e0, pair)].reshape(pair * ff, width)
+        return (lax.dot_general(w[:, :wide], tok_scr[0], nt, preferred_element_type=jnp.float32)
+                + lax.dot_general(w[:, wide:], tok_scr[1], nt, preferred_element_type=jnp.float32))
+
+    def step(j, carry):
+        e0 = j * pair
+        for e in range(pair):
+            for k, ref in enumerate((wg_ref, wu_ref, wd_ref)):
+                fetch(e0 + e, k, ref).wait()
+        gate = both(0, e0, x_scr).reshape(pair, ff, rows)
+        up = both(1, e0, x_scr).reshape(pair, ff, rows)
+        back = both(2, e0, g_scr).reshape(pair, ff, rows)
+        ct = ct_scr[pl.ds(h * (exp_own * n_group) + base + e0, pair), :].reshape(pair, 1, rows)
+        sig = jax.nn.sigmoid(gate)
+        silu = gate * sig
+        d_hid = back * ct
+        hid = (silu * up * ct).astype(jnp.bfloat16)
+        d_up = (d_hid * silu).astype(jnp.bfloat16)
+        d_gate = (d_hid * up * sig * (1.0 + gate * (1.0 - sig))).astype(jnp.bfloat16)
+        where_l = lax.broadcasted_iota(jnp.int32, (ff, exp_own * slots), 1) // slots
+        for k, val in enumerate((d_gate, d_up, hid)):
+            for e in range(pair):
+                packed = jnp.dot(val[e], picks[0], preferred_element_type=jnp.float32)
+                act_scr[k] = jnp.where(where_l == e0 + e, packed, act_scr[k])
+        w = [wbuf[k, pl.ds(e0, pair)].reshape(pair * ff, width) for k in range(3)]
+        flat = [val.reshape(pair * ff, rows) for val in (d_gate, d_up, hid)]
+        acc_o[...] += lax.dot_general(flat[2], w[2], tn, preferred_element_type=jnp.float32)
+        acc_i[...] += (lax.dot_general(flat[0], w[0], tn, preferred_element_type=jnp.float32)
+                       + lax.dot_general(flat[1], w[1], tn, preferred_element_type=jnp.float32))
+        return carry
+
+    lax.fori_loop(0, exp_own // pair, step, 0)
+    act_ref[...] = act_scr[...].astype(jnp.bfloat16)
+    narrow = width // n_ingroup
+    for q in range(n_ingroup):
+        for b in range(n_group * n_hid):
+            rel_i = q ^ i
+            rel_b = b ^ (g * n_hid + h)
+            cols = slice(q * narrow, (q + 1) * narrow)
+            at = slice(b * tok, (b + 1) * tok)
+            part_ref[lax.rem(rel_i, 2), rel_i // 2, rel_b, 0] = acc_o[at, cols].astype(jnp.bfloat16)
+            part_ref[lax.rem(rel_i, 2), rel_i // 2, rel_b, 1] = acc_i[at, cols].astype(jnp.bfloat16)
+
+
+def grad_kernel(slots, first, scal, act_ref, xs_ref, gs_ref, *refs):
+    gate_ref, up_ref, down_ref = refs[-3:]
+    j = pl.program_id(0) + first
+    where_l = lax.broadcasted_iota(jnp.int32, act_ref.shape[1:], 1) // slots
+    for k, (out, right) in enumerate(((gate_ref, xs_ref), (up_ref, xs_ref), (down_ref, gs_ref))):
+        left = jnp.where(where_l == j, act_ref[k], jnp.zeros((), jnp.bfloat16))
+        out[0] = jnp.dot(left, right[...], preferred_element_type=jnp.float32)
+
+
+def grads(scal, act, xs, gs, which, first, count, before, experts, n_group, slots):
+    ff = act.shape[1]
+    wide = xs.shape[2]
+    own = experts // n_group
+
+    def out_map(j, scal):
+        return (lax.rem(scal[0] + which, n_group) * own + first + j, 0, 0)
+
+    full = jax.ShapeDtypeStruct((experts, ff, wide), jnp.float32)
+    n_before = 3 if before is not None else 0
+    return pl.pallas_call(
+        functools.partial(grad_kernel, slots, first),
+        out_shape=[full] * 3,
+        grid_spec=pltpu.PrefetchScalarGridSpec(
+            num_scalar_prefetch=1,
+            grid=(count,),
+            in_specs=[
+                pl.BlockSpec(act.shape, lambda j, scal: (0, 0, 0)),
+                pl.BlockSpec((None,) + xs.shape[1:], lambda j, scal: (which, 0, 0)),
+                pl.BlockSpec((None,) + gs.shape[1:], lambda j, scal: (which, 0, 0)),
+            ] + [pl.BlockSpec(memory_space=pl.ANY)] * n_before,
+            out_specs=[pl.BlockSpec((1, ff, wide), out_map)] * 3,
+        ),
+        input_output_aliases={4 + k: k for k in range(n_before)},
+        compiler_params=pltpu.CompilerParams(vmem_limit_bytes=40 << 20),
+        cost_estimate=pl.CostEstimate(
+            flops=count * 3 * 2 * ff * act.shape[2] * wide,
+            bytes_accessed=count * 3 * ff * wide * 4, transcendentals=0),
+        name="weight_grads",
+    )(scal, act, xs, gs, *(before or ()))
+
+
+def swap(x, axis, bit):
+    n = lax.axis_size(axis)
+    return lax.ppermute(x, axis, [(k, k ^ bit) for k in range(n)])
+
+
+def shards(tokens, grad_mixed, expert_ids, gate_weight, w_gate, w_up, w_down):
+    tok, width = tokens.shape
+    n_group, n_ingroup, n_hid = (lax.axis_size(a) for a in ("group", "ingroup", "hid"))
+    exp_dev, ff = w_down.shape[0], w_down.shape[1]
+    experts = exp_dev * n_hid
+    cap = tok // 8
+    own = exp_dev // n_group
+    rows = n_group * n_hid * tok
+    slots = n_group * n_hid * cap
+    if not (n_group == 2 and n_ingroup == 4 and exp_dev % (2 * n_group) == 0 and n_hid & (n_hid - 1) == 0
+            and rows == 128 and own * slots == 128 and 2 * experts <= 128):
+        return plain(tokens, grad_mixed, expert_ids, gate_weight, w_gate, w_up, w_down)
+    g, i, h = (lax.axis_index(a) for a in ("group", "ingroup", "hid"))
+    scal = jnp.stack([g, i, h]).astype(jnp.int32)
+    core = lax.rem(i, 2)
+    half = width // 2
+    table = jnp.sum(jnp.where(expert_ids[:, :, None] == jnp.arange(experts, dtype=jnp.int32)[None, None, :],
+                              gate_weight[:, :, None], 0.0), axis=1)
+    hi = lax.reduce_precision(table, 8, 7)
+    mid = lax.reduce_precision(table - hi, 8, 7)
+    low = lax.reduce_precision(table - hi - mid, 8, 7)
+    zero = jnp.zeros_like(hi)
+    terms = jnp.where(core == 0, jnp.concatenate([hi, mid], 1), jnp.concatenate([low, zero], 1))
+    message = jnp.concatenate([
+        lax.dynamic_slice_in_dim(tokens, core * half, half, 1),
+        lax.dynamic_slice_in_dim(grad_mixed, core * half, half, 1),
+        terms.astype(jnp.bfloat16)], axis=1)
+    line = [message] + [lax.ppermute(message, "hid", [(k, (k + d) % n_hid) for k in range(n_hid)])
+                        for d in range(1, n_hid)]
+    line = jnp.stack(line)
+    mine = jnp.concatenate([line, swap(line, "group", 1)])
+    theirs = swap(mine, "ingroup", 1)
+    wg, wu = jnp.swapaxes(w_gate, 1, 2), jnp.swapaxes(w_up, 1, 2)
+    narrow = width // n_ingroup
+    any_space = pl.BlockSpec(memory_space=pl.ANY)
+    vmem = pl.BlockSpec(memory_space=pltpu.VMEM)
+    lanes = message.shape[1] - 2 * half
+    part, act, xs, gs = pl.pallas_call(
+        functools.partial(middle_kernel, (n_group, n_ingroup, n_hid, tok, experts, half, cap)),
+        out_shape=[
+            jax.ShapeDtypeStruct((2, n_ingroup // 2, n_group * n_hid, 2, tok, narrow), jnp.bfloat16),
+            jax.ShapeDtypeStruct((3, ff, own * slots), jnp.bfloat16),
+            jax.ShapeDtypeStruct((n_group, own * slots, half), jnp.bfloat16),
+            jax.ShapeDtypeStruct((n_group, own * slots, half), jnp.bfloat16),
+        ],
+        in_specs=[pl.BlockSpec(memory_space=pltpu.SMEM), vmem, vmem, any_space, any_space, any_space],
+        out_specs=[vmem] * 4,
+        scratch_shapes=[
+            pltpu.VMEM((2, rows, half), jnp.bfloat16),
+            pltpu.VMEM((2, rows, half), jnp.bfloat16),
+            pltpu.VMEM((2, rows, lanes), jnp.float32),
+            pltpu.VMEM((lanes, rows), jnp.float32),
+            pltpu.VMEM((3, own, ff, width), jnp.bfloat16),
+            pltpu.VMEM((rows, width), jnp.float32),
+            pltpu.VMEM((rows, width), jnp.float32),
+            pltpu.VMEM((3, ff, own * slots), jnp.float32),
+            pltpu.SemaphoreType.DMA((3, own)),
+        ],
+        compiler_params=pltpu.CompilerParams(vmem_limit_bytes=62 << 20),
+        cost_estimate=pl.CostEstimate(flops=6 * 2 * own * ff * width * rows,
+                                      bytes_accessed=3 * own * ff * width * 2, transcendentals=own * ff * rows),
+        name="experts",
+    )(scal, mine, theirs, wg, wu, w_down)
+    act_other = swap(act, "group", 1)
+    args = (exp_dev, n_group, slots)
+    now = part[0] + swap(part[1], "ingroup", 1)
+    now = now[0] + swap(now[1], "ingroup", 2)
+    span = n_group * n_hid // 2
+    now = now[:span] + swap(now[span:], "group", 1)
+    bit = n_hid // 2
+    while bit:
+        now = now[:bit] + swap(now[bit:], "hid", bit)
+        bit //= 2
+    out = grads(scal, act, xs, gs, 0, 0, own, None, *args)
+    out = grads(scal, act_other, xs, gs, 1, 0, own, out, *args)
+    return (now[0, 0], now[0, 1], jnp.swapaxes(out[0], 1, 2), jnp.swapaxes(out[1], 1, 2), out[2])
+
+
 def solution(mesh):
     placed = (
         P(("group", "hid"), None),

time: 930 us -> 106 us (0.11)
  waiting for transfers between devices: 736 us -> 22.4 us
  matrix products: 98.6 us -> 0 us
  Pallas kernels: 0 us -> 53.8 us
  other arithmetic: 44 us -> 2.78 us
  between operations: 14 us -> 0.77 us
    reduce_scatter x5 -> x0, waiting for transfers between devices: 719 us -> none  [the longest x1 246 us: shards(): lax.psum_scatter(term_up.astype(jnp.bfloat16), 'group', scatter_dimension...]
    dot_general x9 -> x0, matrix products: 98.6 us -> none  [the longest x1 11.5 us: shards(): jnp.einsum('emh,edh->emd', d_up, w_up, preferred_element_type=jnp.float32)]
    pallas_call x0 -> x3, Pallas kernels: none -> 53.8 us  [the longest x1 29.6 us: shards(): pl.pallas_call(functools.partial(middle_kernel, (n_group, n_ingroup, n_hi...]
    convert_element_type x5 -> x1, other arithmetic: 40.9 us -> 0.08 us  [shards(): terms.astype(jnp.bfloat16)]
    ppermute x0 -> x11, waiting for transfers between devices: none -> 22.4 us  [the longest x8 19.6 us: swap(): return lax.ppermute(x, axis, [(k, k ^ bit) for k in range(n)])]
    all_to_all x4 -> x0, starting transfers between devices: 18 us -> none  [the longest x1 6.35 us: shards(): lax.all_to_all(send_x.reshape(shape_whole), 'hid', split_axis=1, concat_a...]
    ppermute x0 -> x11, starting transfers between devices: none -> 17.5 us  [the longest x8 9.54 us: swap(): return lax.ppermute(x, axis, [(k, k ^ bit) for k in range(n)])]
    all_to_all x4 -> x0, waiting for transfers between devices: 16.7 us -> none  [the longest x1 7.6 us: shards(): lax.all_to_all(send_x.reshape(shape_whole), 'hid', split_axis=1, concat_a...]
  transfers between devices with their start and end apart: 9 -> 11, of which waited for: 6 -> 8; matrix products, arithmetic and copies ran while one was open for 13% -> 1% of each run, Pallas kernels for 0% -> 23%
where the time goes in v1:
time: 106 us
  Pallas kernels  53.8 us (51%)
  waiting for transfers between devices  22.4 us (21%)
  starting transfers between devices  17.5 us (17%)
  local copies, waits for them, and re-layouts  8.51 us (8%)
  other arithmetic  2.78 us (3%)
    pallas_call x1, Pallas kernels, shards(): pl.pallas_call(functools.partial(middle_kernel, (n_group, n_ingroup, n_hi...  29.6 us
    pallas_call x2, Pallas kernels, grads(): pl.pallas_call(functools.partial(grad_kernel, slots, first), out_shape=[f...  24.2 us
    ppermute x8, waiting for transfers between devices, swap(): return lax.ppermute(x, axis, [(k, k ^ bit) for k in range(n)])  19.6 us
    ppermute x8, starting transfers between devices, swap(): return lax.ppermute(x, axis, [(k, k ^ bit) for k in range(n)])  9.54 us
    ppermute x3, starting transfers between devices, shards(): lax.ppermute(message, 'hid', [(k, (k + d) % n_hid) for k in range(n_hid)])  7.95 us
    unnamed x19, local copies, waits for them, and re-layouts  5.96 us
    ppermute x3, waiting for transfers between devices, shards(): lax.ppermute(message, 'hid', [(k, (k + d) % n_hid) for k in range(n_hid)])  2.8 us
  transfers between devices with their start and end apart: 11, of which 8 were waited for; matrix products, arithmetic and copies ran while one was open for 1% of the time, Pallas kernels for 23%

profile of v1, /device:TPU:0, one launch (start us, length us, event | category | flops | bytes accessed | tf_op | source)
XLA Modules:
  0.0 105.8 jit_solution(16081858782772857016)
XLA Ops:
  2.3 4.1 %collective-permute-start.1 = (bf16[16,2176]{1,0:T(8,128)(2,1)S(1)}, bf16[16,2176]{1,0:T(8,128)(2,1)S(1)}, u32[]{:S(2)}, u32[]{:S(2)}) collective-permute-start(bf16[16,2176]{1,0:T(8,128)(2,1)S(1)} %get-tuple-element.26), channel_id=1, source_target_pairs={{0,2},{1,3},{2,0},{3,1},{4,6},{5,7},{6,4},{7,5},{8,10},{9,11},{10,... | collective-permute-start | bytes 208904 | tf_op jit(solution)/shard_map/ppermute | solution.py:281
  6.5 1.6 %collective-permute-start = (bf16[16,2176]{1,0:T(8,128)(2,1)S(1)}, bf16[16,2176]{1,0:T(8,128)(2,1)S(1)}, u32[]{:S(2)}, u32[]{:S(2)}) collective-permute-start(bf16[16,2176]{1,0:T(8,128)(2,1)S(1)} %get-tuple-element.26), channel_id=1, source_target_pairs={{0,1},{1,2},{2,3},{3,0},{4,5},{5,6},{6,7},{7,4},{8,9},{9,10},{10,1... | collective-permute-start | bytes 208904 | tf_op jit(solution)/shard_map/ppermute | solution.py:281
  8.1 2.2 %collective-permute-start.2 = (bf16[16,2176]{1,0:T(8,128)(2,1)S(1)}, bf16[16,2176]{1,0:T(8,128)(2,1)S(1)}, u32[]{:S(2)}, u32[]{:S(2)}) collective-permute-start(bf16[16,2176]{1,0:T(8,128)(2,1)S(1)} %get-tuple-element.26), channel_id=1, source_target_pairs={{0,3},{1,0},{2,1},{3,2},{4,7},{5,4},{6,5},{7,6},{8,11},{9,8},{10,9... | collective-permute-start | bytes 208904 | tf_op jit(solution)/shard_map/ppermute | solution.py:281
  10.4 2.4 %collective-permute-done = bf16[16,2176]{1,0:T(8,128)(2,1)S(1)} collective-permute-done((bf16[16,2176]{1,0:T(8,128)(2,1)S(1)}, bf16[16,2176]{1,0:T(8,128)(2,1)S(1)}, u32[]{:S(2)}, u32[]{:S(2)}) %collective-permute-start) | collective-permute-done | bytes 69664 | tf_op jit(solution)/shard_map/ppermute | solution.py:281
  13.2 1.7 %collective-permute-start.3 = (bf16[4,16,2176]{2,1,0:T(8,128)(2,1)S(1)}, bf16[4,16,2176]{2,1,0:T(8,128)(2,1)S(1)}, u32[]{:S(2)}, u32[]{:S(2)}) collective-permute-start(bf16[4,16,2176]{2,1,0:T(8,128)(2,1)S(1)} %pad_maximum_fusion), channel_id=1, source_target_pairs={{0,16},{16,0},{1,17},{17,1},{2,18},{18,2},{3,19},{19,3},{4,20},{20... | collective-permute-start | bytes 835592 | tf_op jit(solution)/shard_map/ppermute | solution.py:251
  14.9 5.6 %collective-permute-done.3 = bf16[4,16,2176]{2,1,0:T(8,128)(2,1)S(1)} collective-permute-done((bf16[4,16,2176]{2,1,0:T(8,128)(2,1)S(1)}, bf16[4,16,2176]{2,1,0:T(8,128)(2,1)S(1)}, u32[]{:S(2)}, u32[]{:S(2)}) %collective-permute-start.3) | collective-permute-done | bytes 278560 | tf_op jit(solution)/shard_map/ppermute | solution.py:251
  21.3 1.3 %collective-permute-done.4.v_ref = bf16[8,16,2176]{2,1,0:T(8,128)(2,1)S(1)} collective-permute-done((bf16[8,16,2176]{2,1,0:T(8,128)(2,1)S(1)}, bf16[8,16,2176]{2,1,0:T(8,128)(2,1)S(1)}, u32[]{:S(2)}, u32[]{:S(2)}) %collective-permute-start.4) | collective-permute-done | bytes 557088 | tf_op jit(solution)/shard_map/ppermute | solution.py:251
  22.6 0.8 copy-done.7
  23.4 29.6 %experts.1 = (bf16[2,2,8,2,16,512]{5,4,3,2,1,0:T(8,128)(2,1)}, bf16[3,352,128]{2,1,0:T(8,128)(2,1)}, bf16[2,128,1024]{2,1,0:T(8,128)(2,1)}, bf16[2,128,1024]{2,1,0:T(8,128)(2,1)}) custom-call(s32[3]{0:T(128)} %pad_add_fusion.scal, bf16[8,16,2176]{2,1,0:T(8,128)(2,1)} %copy-done.6, bf16[8,16,2176]{2,1,0:T(8,128)(2,1)} %copy-done.7, ...), custom_call_target="tpu_custom_call" | custom-call | flops 8858370048 | bytes 34603008 | tf_op jit(solution)/shard_map/experts/pallas_call | solution.py:291
  53.0 1.1 %slice_bitcast_fusion = bf16[2,8,2,16,512]{4,3,2,1,0:T(8,128)(2,1)S(1)} fusion(bf16[2,2,8,2,16,512]{5,4,3,2,1,0:T(8,128)(2,1)} %get-tuple-element.15), kind=kLoop, calls=%fused_computation.1 | loop fusion | bytes 1048576 | tf_op jit(solution)/shard_map/squeeze | solution.py:319
  54.3 1.8 %collective-permute-done.5 = bf16[2,8,2,16,512]{4,3,2,1,0:T(8,128)(2,1)S(1)} collective-permute-done((bf16[2,8,2,16,512]{4,3,2,1,0:T(8,128)(2,1)S(1)}, bf16[2,8,2,16,512]{4,3,2,1,0:T(8,128)(2,1)S(1)}, u32[]{:S(2)}, u32[]{:S(2)}) %collective-permute-start.5) | collective-permute-done | bytes 524320 | tf_op jit(solution)/shard_map/ppermute | solution.py:251
  56.1 1.1 %bitcast_add_fusion = bf16[2,8,2,16,512]{4,3,2,1,0:T(8,128)(2,1)S(1)} fusion(bf16[2,8,2,16,512]{4,3,2,1,0:T(8,128)(2,1)S(1)} %collective-permute-done.5, bf16[2,2,8,2,16,512]{5,4,3,2,1,0:T(8,128)(2,1)} %get-tuple-element.15), kind=kLoop, calls=%fused_computation | loop fusion | flops 262144 | bytes 1572864 | tf_op jit(solution)/shard_map/add | solution.py:319
  57.2 1.8 %collective-permute-start.6 = (bf16[8,2,16,512]{3,2,1,0:T(8,128)(2,1)S(1)}, bf16[8,2,16,512]{3,2,1,0:T(8,128)(2,1)S(1)}, u32[]{:S(2)}, u32[]{:S(2)}) collective-permute-start(bf16[8,2,16,512]{3,2,1,0:T(8,128)(2,1)S(1)} %slice_bitcast_fusion.1), channel_id=1, source_target_pairs={{0,8},{4,12},{8,0},{12,4},{1,9},{5,13},{9,1},{13,5},{2,10},{6,14},... | collective-permute-start | bytes 786440 | tf_op jit(solution)/shard_map/ppermute | solution.py:251
  59.1 6.6 %collective-permute-done.6 = bf16[8,2,16,512]{3,2,1,0:T(8,128)(2,1)S(1)} collective-permute-done((bf16[8,2,16,512]{3,2,1,0:T(8,128)(2,1)S(1)}, bf16[8,2,16,512]{3,2,1,0:T(8,128)(2,1)S(1)}, u32[]{:S(2)}, u32[]{:S(2)}) %collective-permute-start.6) | collective-permute-done | bytes 262176 | tf_op jit(solution)/shard_map/ppermute | solution.py:251
  65.7 1.8 %collective-permute-start.7 = (bf16[4,2,16,512]{3,2,1,0:T(8,128)(2,1)S(1)}, bf16[4,2,16,512]{3,2,1,0:T(8,128)(2,1)S(1)}, u32[]{:S(2)}, u32[]{:S(2)}) collective-permute-start(bf16[4,2,16,512]{3,2,1,0:T(8,128)(2,1)S(1)} %slice.51), channel_id=1, source_target_pairs={{0,16},{16,0},{1,17},{17,1},{2,18},{18,2},{3,19},{19,3},{4,20},{20... | collective-permute-start | bytes 393224 | tf_op jit(solution)/shard_map/ppermute | solution.py:251
  67.8 4.3 %collective-permute-done.7 = bf16[4,2,16,512]{3,2,1,0:T(8,128)(2,1)S(1)} collective-permute-done((bf16[4,2,16,512]{3,2,1,0:T(8,128)(2,1)S(1)}, bf16[4,2,16,512]{3,2,1,0:T(8,128)(2,1)S(1)}, u32[]{:S(2)}, u32[]{:S(2)}) %collective-permute-start.7) | collective-permute-done | bytes 131104 | tf_op jit(solution)/shard_map/ppermute | solution.py:251
  72.2 2.9 %collective-permute-start.8 = (bf16[2,2,16,512]{3,2,1,0:T(8,128)(2,1)S(1)}, bf16[2,2,16,512]{3,2,1,0:T(8,128)(2,1)S(1)}, u32[]{:S(2)}, u32[]{:S(2)}) collective-permute-start(bf16[2,2,16,512]{3,2,1,0:T(8,128)(2,1)S(1)} %slice.53), channel_id=1, source_target_pairs={{0,2},{1,3},{2,0},{3,1},{4,6},{5,7},{6,4},{7,5},{8,10},{9,11},{10,... | collective-permute-start | bytes 196616 | tf_op jit(solution)/shard_map/ppermute | solution.py:251
  75.1 1.0 copy-done
  76.2 1.0 copy-done.2
  77.2 1.0 copy-done.5
  78.2 12.1 %weight_grads.2 = (f32[16,352,1024]{2,1,0:T(8,128)}, f32[16,352,1024]{2,1,0:T(8,128)}, f32[16,352,1024]{2,1,0:T(8,128)}) custom-call(s32[3]{0:T(128)S(1)} %copy-done.4, bf16[3,352,128]{2,1,0:T(8,128)(2,1)S(1)} %copy-done.5, bf16[2,128,1024]{2,1,0:T(8,128)(2,1)S(1)} %copy-done, bf16[2,128,1024]{2,1,0:T(8,128)(2,1)S(1)} %copy-done.2), custom_call_target="tpu_custom_call" | custom-call | flops 2214592512 | bytes 34603008 | tf_op jit(solution)/shard_map/weight_grads/pallas_call | solution.py:227
  91.0 1.0 copy-done.1
  92.1 1.0 copy-done.3
  93.1 12.1 %weight_grads.3 = (f32[16,352,1024]{2,1,0:T(8,128)}, f32[16,352,1024]{2,1,0:T(8,128)}, f32[16,352,1024]{2,1,0:T(8,128)}) custom-call(s32[3]{0:T(128)S(1)} %copy-done.4, bf16[3,352,128]{2,1,0:T(8,128)(2,1)S(1)} %collective-permute-done.10.act_ref, bf16[2,128,1024]{2,1,0:T(8,128)(2,1)S(1)} %copy-done.1, ...), custom_call_target="tpu_custom_call", output_to_operand_aliasing={{0}: (4, {}), {1}: (5, {}), {2}: (6, {})} | custom-call | flops 2214592512 | bytes 34603008 | tf_op jit(solution)/shard_map/weight_grads/pallas_call | solution.py:227
  (40 shorter events, 4.9 us)
Async XLA Ops:
  2.3 8.1 %collective-permute-start.1 = (bf16[16,2176]{1,0:T(8,128)(2,1)S(1)}, bf16[16,2176]{1,0:T(8,128)(2,1)S(1)}, u32[]{:S(2)}, u32[]{:S(2)}) collective-permute-start(bf16[16,2176]{1,0:T(8,128)(2,1)S(1)} %get-tuple-element.26), channel_id=1, source_target_pairs={{0,2},{1,3},{2,0},{3,1},{4,6},{5,7},{6,4},{7,5},{8,10},{9,11},{10,... | collective-permute-start | bytes 208904 | tf_op jit(solution)/shard_map/ppermute | solution.py:281
  6.5 6.3 %collective-permute-start = (bf16[16,2176]{1,0:T(8,128)(2,1)S(1)}, bf16[16,2176]{1,0:T(8,128)(2,1)S(1)}, u32[]{:S(2)}, u32[]{:S(2)}) collective-permute-start(bf16[16,2176]{1,0:T(8,128)(2,1)S(1)} %get-tuple-element.26), channel_id=1, source_target_pairs={{0,1},{1,2},{2,3},{3,0},{4,5},{5,6},{6,7},{7,4},{8,9},{9,10},{10,1... | collective-permute-start | bytes 208904 | tf_op jit(solution)/shard_map/ppermute | solution.py:281
  8.1 5.1 %collective-permute-start.2 = (bf16[16,2176]{1,0:T(8,128)(2,1)S(1)}, bf16[16,2176]{1,0:T(8,128)(2,1)S(1)}, u32[]{:S(2)}, u32[]{:S(2)}) collective-permute-start(bf16[16,2176]{1,0:T(8,128)(2,1)S(1)} %get-tuple-element.26), channel_id=1, source_target_pairs={{0,3},{1,0},{2,1},{3,2},{4,7},{5,4},{6,5},{7,6},{8,11},{9,8},{10,9... | collective-permute-start | bytes 208904 | tf_op jit(solution)/shard_map/ppermute | solution.py:281
  13.2 7.4 %collective-permute-start.3 = (bf16[4,16,2176]{2,1,0:T(8,128)(2,1)S(1)}, bf16[4,16,2176]{2,1,0:T(8,128)(2,1)S(1)}, u32[]{:S(2)}, u32[]{:S(2)}) collective-permute-start(bf16[4,16,2176]{2,1,0:T(8,128)(2,1)S(1)} %pad_maximum_fusion), channel_id=1, source_target_pairs={{0,16},{16,0},{1,17},{17,1},{2,18},{18,2},{3,19},{19,3},{4,20},{20... | collective-permute-start | bytes 835592 | tf_op jit(solution)/shard_map/ppermute | solution.py:251
  20.6 2.0 %copy-start.6 = (bf16[8,16,2176]{2,1,0:T(8,128)(2,1)}, bf16[8,16,2176]{2,1,0:T(8,128)(2,1)S(1)}, u32[]{:S(2)}) copy-start(bf16[8,16,2176]{2,1,0:T(8,128)(2,1)S(1)} %constant_dynamic-update-slice_fusion.u_ref) | copy-start | bytes 1671172
  20.6 2.0 %collective-permute-start.4 = (bf16[8,16,2176]{2,1,0:T(8,128)(2,1)S(1)}, bf16[8,16,2176]{2,1,0:T(8,128)(2,1)S(1)}, u32[]{:S(2)}, u32[]{:S(2)}) collective-permute-start(bf16[8,16,2176]{2,1,0:T(8,128)(2,1)S(1)} %constant_dynamic-update-slice_fusion.u_ref), channel_id=1, source_target_pairs={{0,4},{4,0},{8,12},{12,8},{1,5},{5,1},{9,13},{13,9},{2,6},{6,2},{1... | collective-permute-start | bytes 1671176 | tf_op jit(solution)/shard_map/ppermute | solution.py:251
  22.6 0.8 copy-start.7
  23.4 51.7 %copy-start.4 = (s32[3]{0:T(128)S(1)}, s32[3]{0:T(128)}, u32[]{:S(2)}) copy-start(s32[3]{0:T(128)} %pad_add_fusion.scal) | copy-start | bytes 40
  54.1 2.0 %collective-permute-start.5 = (bf16[2,8,2,16,512]{4,3,2,1,0:T(8,128)(2,1)S(1)}, bf16[2,8,2,16,512]{4,3,2,1,0:T(8,128)(2,1)S(1)}, u32[]{:S(2)}, u32[]{:S(2)}) collective-permute-start(bf16[2,8,2,16,512]{4,3,2,1,0:T(8,128)(2,1)S(1)} %slice_bitcast_fusion), channel_id=1, source_target_pairs={{0,4},{4,0},{8,12},{12,8},{1,5},{5,1},{9,13},{13,9},{2,6},{6,2},{1... | collective-permute-start | bytes 1572872 | tf_op jit(solution)/shard_map/ppermute | solution.py:251
  57.2 8.4 %collective-permute-start.6 = (bf16[8,2,16,512]{3,2,1,0:T(8,128)(2,1)S(1)}, bf16[8,2,16,512]{3,2,1,0:T(8,128)(2,1)S(1)}, u32[]{:S(2)}, u32[]{:S(2)}) collective-permute-start(bf16[8,2,16,512]{3,2,1,0:T(8,128)(2,1)S(1)} %slice_bitcast_fusion.1), channel_id=1, source_target_pairs={{0,8},{4,12},{8,0},{12,4},{1,9},{5,13},{9,1},{13,5},{2,10},{6,14},... | collective-permute-start | bytes 786440 | tf_op jit(solution)/shard_map/ppermute | solution.py:251
  65.7 6.4 %collective-permute-start.7 = (bf16[4,2,16,512]{3,2,1,0:T(8,128)(2,1)S(1)}, bf16[4,2,16,512]{3,2,1,0:T(8,128)(2,1)S(1)}, u32[]{:S(2)}, u32[]{:S(2)}) collective-permute-start(bf16[4,2,16,512]{3,2,1,0:T(8,128)(2,1)S(1)} %slice.51), channel_id=1, source_target_pairs={{0,16},{16,0},{1,17},{17,1},{2,18},{18,2},{3,19},{19,3},{4,20},{20... | collective-permute-start | bytes 393224 | tf_op jit(solution)/shard_map/ppermute | solution.py:251
  67.5 23.5 %collective-permute-start.10 = (bf16[3,352,128]{2,1,0:T(8,128)(2,1)}, bf16[3,352,128]{2,1,0:T(8,128)(2,1)S(1)}, u32[]{:S(2)}, u32[]{:S(2)}) collective-permute-start(bf16[3,352,128]{2,1,0:T(8,128)(2,1)} %get-tuple-element.16.act_ref), channel_id=1, source_target_pairs={{0,16},{16,0},{1,17},{17,1},{2,18},{18,2},{3,19},{19,3},{4,20},{20... | collective-permute-start | bytes 811016 | tf_op jit(solution)/shard_map/ppermute | solution.py:251
  72.2 18.1 %collective-permute-start.8 = (bf16[2,2,16,512]{3,2,1,0:T(8,128)(2,1)S(1)}, bf16[2,2,16,512]{3,2,1,0:T(8,128)(2,1)S(1)}, u32[]{:S(2)}, u32[]{:S(2)}) collective-permute-start(bf16[2,2,16,512]{3,2,1,0:T(8,128)(2,1)S(1)} %slice.53), channel_id=1, source_target_pairs={{0,2},{1,3},{2,0},{3,1},{4,6},{5,7},{6,4},{7,5},{8,10},{9,11},{10,... | collective-permute-start | bytes 196616 | tf_op jit(solution)/shard_map/ppermute | solution.py:251
  75.1 1.0 copy-start
  76.2 1.0 copy-start.2
  77.2 1.0 copy-start.5
  90.3 14.9 %collective-permute-start.9 = (bf16[1,2,16,512]{3,2,1,0:T(8,128)(2,1)S(1)}, bf16[1,2,16,512]{3,2,1,0:T(8,128)(2,1)S(1)}, u32[]{:S(2)}, u32[]{:S(2)}) collective-permute-start(bf16[1,2,16,512]{3,2,1,0:T(8,128)(2,1)S(1)} %slice.55), channel_id=1, source_target_pairs={{0,1},{1,0},{2,3},{3,2},{4,5},{5,4},{6,7},{7,6},{8,9},{9,8},{10,11... | collective-permute-start | bytes 98312 | tf_op jit(solution)/shard_map/ppermute | solution.py:251
  91.0 1.0 copy-start.1
  92.1 1.0 copy-start.3

commit v2 on v1

--- a/solution.py
+++ b/solution.py
@@ -96,10 +96,11 @@
     return (mixed, grad_tokens, grad_gate, grad_up, grad_down)
 
 
-def middle_kernel(sizes, scal, u_ref, v_ref, wg_ref, wu_ref, wd_ref,
-                  part_ref, act_ref, xs_ref, gs_ref,
-                  x_scr, g_scr, c_scr, ct_scr, wbuf, acc_o, acc_i, act_scr, sem):
+def middle_kernel(sizes, places, scal, wg_ref, wu_ref, wd_ref, *refs):
     n_group, n_ingroup, n_hid, tok, experts, half, cap = sizes
+    message_refs, refs = refs[:2 * len(places)], refs[2 * len(places):]
+    keep_ref, send_ref, act_ref, xs_ref, gs_ref = refs[:5]
+    x_scr, g_scr, c_scr, w_scr, pick_scr, wbuf, acc_o, acc_i, sem = refs[5:]
     ff, width = wbuf.shape[2], wbuf.shape[3]
     exp_own = wbuf.shape[1]
     rows = n_group * n_hid * tok
@@ -107,29 +108,32 @@
     g, i, h = scal[0], scal[1], scal[2]
     core = lax.rem(i, 2)
     base = g * exp_own
+    pair = 2
 
     def fetch(e, k, ref):
         return pltpu.make_async_copy(ref.at[base + e], wbuf.at[k, e], sem.at[k, e])
 
-    for e in range(exp_own):
+    for e0 in range(0, exp_own, pair):
         for k, ref in enumerate((wg_ref, wu_ref, wd_ref)):
-            fetch(e, k, ref).start()
-
-    for ref, part in ((u_ref, core), (v_ref, 1 - core)):
-        for s in range(n_group):
-            for d in range(n_hid):
+            for e in range(pair):
+                fetch(e0 + e, k, ref).start()
+
+    for m, place in enumerate(places):
+        for ref, part in ((message_refs[2 * m], core), (message_refs[2 * m + 1], 1 - core)):
+            for at_msg, (s, d) in enumerate(place):
                 block = lax.rem(g + s, n_group) * n_hid + lax.rem(h - d + n_hid, n_hid)
                 at = pl.ds(pl.multiple_of(block * tok, tok), tok)
-                msg = s * n_hid + d
-                x_scr[part, at, :] = ref[msg, :, :wide]
-                g_scr[part, at, :] = ref[msg, :, wide:2 * wide]
-                c_scr[part, at, :] = ref[msg, :, 2 * wide:].astype(jnp.float32)
+                cols = pl.ds(pl.multiple_of(part * wide, wide), wide)
+                x_scr[at, cols] = ref[at_msg, :, :wide]
+                g_scr[at, cols] = ref[at_msg, :, wide:2 * wide]
+                c_scr[part, at, :] = ref[at_msg, :, 2 * wide:].astype(jnp.float32)
 
     lanes = c_scr.shape[2]
     first, second = c_scr[0], c_scr[1]
     weight = first + pltpu.roll(first, lanes - experts, 1) + second
     lane = lax.broadcasted_iota(jnp.int32, (rows, lanes), 1)
     weight = jnp.where(lane < experts, weight, 0.0)
+    w_scr[...] = weight
     routed = (weight > 0).astype(jnp.bfloat16)
     row_a = lax.broadcasted_iota(jnp.int32, (rows, rows), 0)
     row_b = lax.broadcasted_iota(jnp.int32, (rows, rows), 1)
@@ -137,113 +141,138 @@
     rank = jnp.dot(before, routed, preferred_element_type=jnp.float32)
     block_of = (lax.broadcasted_iota(jnp.int32, (rows, lanes), 0) // tok).astype(jnp.float32)
     slot = jnp.where(weight > 0, rank + cap * block_of, -1.0)
-    ct_scr[...] = weight.T
     slots = n_group * n_hid * cap
     spread_e = lax.broadcasted_iota(jnp.int32, (lanes, exp_own * slots), 0)
     spread_l = lax.broadcasted_iota(jnp.int32, (lanes, exp_own * slots), 1)
     lane_s = lax.broadcasted_iota(jnp.int32, (rows, exp_own * slots), 1)
-    picks = []
     for which in range(n_group):
         owner = h * (exp_own * n_group) + lax.rem(g + which, n_group) * exp_own
         spread = (spread_e == owner + spread_l // slots).astype(jnp.bfloat16)
         slot_l = jnp.dot(slot.astype(jnp.bfloat16), spread, preferred_element_type=jnp.float32)
-        pick = (slot_l == (lane_s % slots).astype(jnp.float32)).astype(jnp.float32)
-        pick_t = pick.T.astype(jnp.bfloat16)
-        picks.append(pick.astype(jnp.bfloat16))
-        xs_ref[which] = jnp.dot(pick_t, x_scr[g], preferred_element_type=jnp.float32).astype(jnp.bfloat16)
-        gs_ref[which] = jnp.dot(pick_t, g_scr[g], preferred_element_type=jnp.float32).astype(jnp.bfloat16)
+        pick = (slot_l == (lane_s % slots).astype(jnp.float32)).astype(jnp.float32).T.astype(jnp.bfloat16)
+        if which == 0:
+            pick_scr[...] = pick
+        xs_ref[which] = jnp.dot(pick, x_scr[:, pl.ds(pl.multiple_of(g * wide, wide), wide)],
+                                preferred_element_type=jnp.float32).astype(jnp.bfloat16)
+        gs_ref[which] = jnp.dot(pick, g_scr[:, pl.ds(pl.multiple_of(g * wide, wide), wide)],
+                                preferred_element_type=jnp.float32).astype(jnp.bfloat16)
 
     acc_o[...] = jnp.zeros_like(acc_o)
     acc_i[...] = jnp.zeros_like(acc_i)
-    act_scr[...] = jnp.zeros_like(act_scr)
-    pair = 2
     nt = (((1,), (1,)), ((), ()))
-    tn = (((0,), (0,)), ((), ()))
-
-    def both(k, e0, tok_scr):
-        w = wbuf[k, pl.ds(e0, pair)].reshape(pair * ff, width)
-        return (lax.dot_general(w[:, :wide], tok_scr[0], nt, preferred_element_type=jnp.float32)
-                + lax.dot_general(w[:, wide:], tok_scr[1], nt, preferred_element_type=jnp.float32))
+    lane_f = lax.broadcasted_iota(jnp.int32, (rows, pair * ff), 1)
 
     def step(j, carry):
         e0 = j * pair
-        for e in range(pair):
-            for k, ref in enumerate((wg_ref, wu_ref, wd_ref)):
+        w, pre = [], []
+        for k, (ref, rows_of) in enumerate(((wg_ref, x_scr), (wu_ref, x_scr), (wd_ref, g_scr))):
+            for e in range(pair):
                 fetch(e0 + e, k, ref).wait()
-        gate = both(0, e0, x_scr).reshape(pair, ff, rows)
-        up = both(1, e0, x_scr).reshape(pair, ff, rows)
-        back = both(2, e0, g_scr).reshape(pair, ff, rows)
-        ct = ct_scr[pl.ds(h * (exp_own * n_group) + base + e0, pair), :].reshape(pair, 1, rows)
+            w.append(wbuf[k, pl.ds(e0, pair)].reshape(pair * ff, width))
+            pre.append(lax.dot_general(rows_of[...], w[k], nt, preferred_element_type=jnp.float32))
+        gate, up, back = pre
+        at = h * (exp_own * n_group) + base + e0
+        col = [jnp.sum(jnp.where(lane == at + e, w_scr[...], 0.0), axis=1, keepdims=True) for e in range(pair)]
+        scale = jnp.where(lane_f < ff, col[0], col[1])
         sig = jax.nn.sigmoid(gate)
         silu = gate * sig
-        d_hid = back * ct
-        hid = (silu * up * ct).astype(jnp.bfloat16)
+        d_hid = back * scale
+        hid = (silu * up * scale).astype(jnp.bfloat16)
         d_up = (d_hid * silu).astype(jnp.bfloat16)
         d_gate = (d_hid * up * sig * (1.0 + gate * (1.0 - sig))).astype(jnp.bfloat16)
-        where_l = lax.broadcasted_iota(jnp.int32, (ff, exp_own * slots), 1) // slots
+        pick = pick_scr[pl.ds(pl.multiple_of(e0 * slots, pair * slots), pair * slots), :]
         for k, val in enumerate((d_gate, d_up, hid)):
+            packed = jnp.dot(pick, val, preferred_element_type=jnp.float32).astype(jnp.bfloat16)
             for e in range(pair):
-                packed = jnp.dot(val[e], picks[0], preferred_element_type=jnp.float32)
-                act_scr[k] = jnp.where(where_l == e0 + e, packed, act_scr[k])
-        w = [wbuf[k, pl.ds(e0, pair)].reshape(pair * ff, width) for k in range(3)]
-        flat = [val.reshape(pair * ff, rows) for val in (d_gate, d_up, hid)]
-        acc_o[...] += lax.dot_general(flat[2], w[2], tn, preferred_element_type=jnp.float32)
-        acc_i[...] += (lax.dot_general(flat[0], w[0], tn, preferred_element_type=jnp.float32)
-                       + lax.dot_general(flat[1], w[1], tn, preferred_element_type=jnp.float32))
+                act_ref[k, pl.ds(pl.multiple_of((e0 + e) * slots, slots), slots), :] = packed[
+                    e * slots:(e + 1) * slots, e * ff:(e + 1) * ff]
+        acc_o[...] += jnp.dot(hid, w[2], preferred_element_type=jnp.float32)
+        acc_i[...] += (jnp.dot(d_gate, w[0], preferred_element_type=jnp.float32)
+                       + jnp.dot(d_up, w[1], preferred_element_type=jnp.float32))
         return carry
 
     lax.fori_loop(0, exp_own // pair, step, 0)
-    act_ref[...] = act_scr[...].astype(jnp.bfloat16)
     narrow = width // n_ingroup
-    for q in range(n_ingroup):
+    for y in range(n_ingroup // 2):
         for b in range(n_group * n_hid):
-            rel_i = q ^ i
+            rel_y = y ^ (i // 2)
             rel_b = b ^ (g * n_hid + h)
-            cols = slice(q * narrow, (q + 1) * narrow)
             at = slice(b * tok, (b + 1) * tok)
-            part_ref[lax.rem(rel_i, 2), rel_i // 2, rel_b, 0] = acc_o[at, cols].astype(jnp.bfloat16)
-            part_ref[lax.rem(rel_i, 2), rel_i // 2, rel_b, 1] = acc_i[at, cols].astype(jnp.bfloat16)
-
-
-def grad_kernel(slots, first, scal, act_ref, xs_ref, gs_ref, *refs):
-    gate_ref, up_ref, down_ref = refs[-3:]
-    j = pl.program_id(0) + first
-    where_l = lax.broadcasted_iota(jnp.int32, act_ref.shape[1:], 1) // slots
-    for k, (out, right) in enumerate(((gate_ref, xs_ref), (up_ref, xs_ref), (down_ref, gs_ref))):
-        left = jnp.where(where_l == j, act_ref[k], jnp.zeros((), jnp.bfloat16))
-        out[0] = jnp.dot(left, right[...], preferred_element_type=jnp.float32)
-
-
-def grads(scal, act, xs, gs, which, first, count, before, experts, n_group, slots):
-    ff = act.shape[1]
-    wide = xs.shape[2]
-    own = experts // n_group
-
-    def out_map(j, scal):
-        return (lax.rem(scal[0] + which, n_group) * own + first + j, 0, 0)
-
-    full = jax.ShapeDtypeStruct((experts, ff, wide), jnp.float32)
-    n_before = 3 if before is not None else 0
+            for k, acc in enumerate((acc_o, acc_i)):
+                two = [acc[at, (2 * y + c) * narrow:(2 * y + c + 1) * narrow].astype(jnp.bfloat16) for c in range(2)]
+                keep_ref[rel_y, rel_b, k] = jnp.where(core == 0, two[0], two[1])
+                send_ref[rel_y, rel_b, k] = jnp.where(core == 0, two[1], two[0])
+
+
+def add_kernel(keep_ref, got_ref, mark_ref, *out_refs):
+    del mark_ref
+    size = out_refs[0].shape[0]
+    for k, out in enumerate(out_refs):
+        at = slice(k * size, (k + 1) * size)
+        out[...] = (keep_ref[at].astype(jnp.float32) + got_ref[at].astype(jnp.float32)).astype(out.dtype)
+
+
+def add_halves(keep, got, mark):
+    vmem = pl.BlockSpec(memory_space=pltpu.VMEM)
+    n = 2 if keep.shape[0] > 1 else 1
     return pl.pallas_call(
-        functools.partial(grad_kernel, slots, first),
-        out_shape=[full] * 3,
-        grid_spec=pltpu.PrefetchScalarGridSpec(
-            num_scalar_prefetch=1,
-            grid=(count,),
-            in_specs=[
-                pl.BlockSpec(act.shape, lambda j, scal: (0, 0, 0)),
-                pl.BlockSpec((None,) + xs.shape[1:], lambda j, scal: (which, 0, 0)),
-                pl.BlockSpec((None,) + gs.shape[1:], lambda j, scal: (which, 0, 0)),
-            ] + [pl.BlockSpec(memory_space=pl.ANY)] * n_before,
-            out_specs=[pl.BlockSpec((1, ff, wide), out_map)] * 3,
-        ),
-        input_output_aliases={4 + k: k for k in range(n_before)},
-        compiler_params=pltpu.CompilerParams(vmem_limit_bytes=40 << 20),
+        add_kernel,
+        out_shape=[jax.ShapeDtypeStruct((keep.shape[0] // n,) + keep.shape[1:], keep.dtype)] * n,
+        in_specs=[vmem, vmem, pl.BlockSpec(memory_space=pl.ANY)],
+        out_specs=[vmem] * n,
+        compiler_params=pltpu.CompilerParams(vmem_limit_bytes=4 << 20),
+        cost_estimate=pl.CostEstimate(flops=keep.size, bytes_accessed=keep.size * 6, transcendentals=0),
+        name="add_halves",
+    )(keep, got, mark)
+
+
+def grad_kernel(piece, slots, n_group, scal, act_ref, xs_ref, gs_ref, *refs):
+    which, first, count = piece
+    *outs, mark_ref, stage, sem = refs[-6:]
+    mark_ref[...] = jnp.zeros_like(mark_ref)
+    own = act_ref.shape[1] // slots
+    base = lax.rem(scal[0] + which, n_group) * own + first
+    tn = (((0,), (0,)), ((), ()))
+    depth = stage.shape[0]
+
+    def put(j, k):
+        slot = lax.rem(j, depth)
+        return pltpu.make_async_copy(stage.at[slot, k], outs[k].at[base + j], sem.at[slot, k])
+
+    def step(j, carry):
+        at = pl.ds(pl.multiple_of((first + j) * slots, slots), slots)
+        for k, right in enumerate((xs_ref, xs_ref, gs_ref)):
+            @pl.when(j >= depth)
+            def _():
+                put(j - depth, k).wait()
+            stage[lax.rem(j, depth), k] = lax.dot_general(
+                act_ref[k, at, :], right[which, at, :], tn, preferred_element_type=jnp.float32)
+            put(j, k).start()
+        return carry
+
+    lax.fori_loop(0, count, step, 0)
+    for j in range(max(0, count - depth), count):
+        for k in range(3):
+            put(j, k).wait()
+
+
+def grads(scal, act, xs, gs, piece, out, after, shape, n_group, slots):
+    ff, wide, count = act.shape[2], xs.shape[2], piece[2]
+    depth = min(2, count)
+    vmem, any_space = pl.BlockSpec(memory_space=pltpu.VMEM), pl.BlockSpec(memory_space=pl.ANY)
+    return pl.pallas_call(
+        functools.partial(grad_kernel, piece, slots, n_group),
+        out_shape=[shape] * 3 + [jax.ShapeDtypeStruct((8, 128), jnp.float32)],
+        in_specs=[pl.BlockSpec(memory_space=pltpu.SMEM)] + [vmem] * 3 + [any_space] * (4 if out else 1),
+        out_specs=[any_space] * 3 + [vmem],
+        scratch_shapes=[pltpu.VMEM((depth, 3, ff, wide), jnp.float32), pltpu.SemaphoreType.DMA((depth, 3))],
+        input_output_aliases={5 + k: k for k in range(3)} if out else {},
+        compiler_params=pltpu.CompilerParams(vmem_limit_bytes=12 << 20),
         cost_estimate=pl.CostEstimate(
-            flops=count * 3 * 2 * ff * act.shape[2] * wide,
+            flops=count * 3 * 2 * ff * slots * wide,
             bytes_accessed=count * 3 * ff * wide * 4, transcendentals=0),
         name="weight_grads",
-    )(scal, act, xs, gs, *(before or ()))
+    )(scal, act, xs, gs, after, *(out or ()))
 
 
 def swap(x, axis, bit):
@@ -280,53 +309,80 @@
         terms.astype(jnp.bfloat16)], axis=1)
     line = [message] + [lax.ppermute(message, "hid", [(k, (k + d) % n_hid) for k in range(n_hid)])
                         for d in range(1, n_hid)]
-    line = jnp.stack(line)
-    mine = jnp.concatenate([line, swap(line, "group", 1)])
-    theirs = swap(mine, "ingroup", 1)
+    messages, places = [], []
+    for low in range(0, n_hid, n_hid // 2):
+        group_of = range(low, low + n_hid // 2)
+        mine = jnp.stack([line[d] for d in group_of])
+        for s, block in enumerate((mine, swap(mine, "group", 1))):
+            messages += [block, swap(block, "ingroup", 1)]
+            places.append(tuple((s, d) for d in group_of))
     wg, wu = jnp.swapaxes(w_gate, 1, 2), jnp.swapaxes(w_up, 1, 2)
     narrow = width // n_ingroup
     any_space = pl.BlockSpec(memory_space=pl.ANY)
     vmem = pl.BlockSpec(memory_space=pltpu.VMEM)
     lanes = message.shape[1] - 2 * half
-    part, act, xs, gs = pl.pallas_call(
-        functools.partial(middle_kernel, (n_group, n_ingroup, n_hid, tok, experts, half, cap)),
+    keep, send, act, xs, gs = pl.pallas_call(
+        functools.partial(middle_kernel, (n_group, n_ingroup, n_hid, tok, experts, half, cap), tuple(places)),
         out_shape=[
-            jax.ShapeDtypeStruct((2, n_ingroup // 2, n_group * n_hid, 2, tok, narrow), jnp.bfloat16),
-            jax.ShapeDtypeStruct((3, ff, own * slots), jnp.bfloat16),
+            jax.ShapeDtypeStruct((n_ingroup // 2, n_group * n_hid, 2, tok, narrow), jnp.bfloat16),
+            jax.ShapeDtypeStruct((n_ingroup // 2, n_group * n_hid, 2, tok, narrow), jnp.bfloat16),
+            jax.ShapeDtypeStruct((3, own * slots, ff), jnp.bfloat16),
             jax.ShapeDtypeStruct((n_group, own * slots, half), jnp.bfloat16),
             jax.ShapeDtypeStruct((n_group, own * slots, half), jnp.bfloat16),
         ],
-        in_specs=[pl.BlockSpec(memory_space=pltpu.SMEM), vmem, vmem, any_space, any_space, any_space],
-        out_specs=[vmem] * 4,
+        in_specs=[pl.BlockSpec(memory_space=pltpu.SMEM)] + [any_space] * 3 + [vmem] * len(messages),
+        out_specs=[vmem] * 5,
         scratch_shapes=[
-            pltpu.VMEM((2, rows, half), jnp.bfloat16),
-            pltpu.VMEM((2, rows, half), jnp.bfloat16),
+            pltpu.VMEM((rows, width), jnp.bfloat16),
+            pltpu.VMEM((rows, width), jnp.bfloat16),
             pltpu.VMEM((2, rows, lanes), jnp.float32),
-            pltpu.VMEM((lanes, rows), jnp.float32),
+            pltpu.VMEM((rows, lanes), jnp.float32),
+            pltpu.VMEM((own * slots, rows), jnp.bfloat16),
             pltpu.VMEM((3, own, ff, width), jnp.bfloat16),
             pltpu.VMEM((rows, width), jnp.float32),
             pltpu.VMEM((rows, width), jnp.float32),
-            pltpu.VMEM((3, ff, own * slots), jnp.float32),
             pltpu.SemaphoreType.DMA((3, own)),
         ],
-        compiler_params=pltpu.CompilerParams(vmem_limit_bytes=62 << 20),
+        compiler_params=pltpu.CompilerParams(vmem_limit_bytes=46 << 20),
         cost_estimate=pl.CostEstimate(flops=6 * 2 * own * ff * width * rows,
                                       bytes_accessed=3 * own * ff * width * 2, transcendentals=own * ff * rows),
         name="experts",
-    )(scal, mine, theirs, wg, wu, w_down)
+    )(scal, wg, wu, w_down, *messages)
+    grad_shape = jax.ShapeDtypeStruct((exp_dev, ff, width // n_group), jnp.float32)
     act_other = swap(act, "group", 1)
-    args = (exp_dev, n_group, slots)
-    now = part[0] + swap(part[1], "ingroup", 1)
-    now = now[0] + swap(now[1], "ingroup", 2)
-    span = n_group * n_hid // 2
-    now = now[:span] + swap(now[span:], "group", 1)
+    rounds = [("ingroup", 1), ("ingroup", 2), ("group", 1)]
     bit = n_hid // 2
     while bit:
-        now = now[:bit] + swap(now[bit:], "hid", bit)
+        rounds.append(("hid", bit))
         bit //= 2
-    out = grads(scal, act, xs, gs, 0, 0, own, None, *args)
-    out = grads(scal, act_other, xs, gs, 1, 0, own, out, *args)
-    return (now[0, 0], now[0, 1], jnp.swapaxes(out[0], 1, 2), jnp.swapaxes(out[1], 1, 2), out[2])
+    weights = [1] * (len(rounds) - 1)
+    pieces = [[]] + cut(own, n_group, weights)
+    out, mark = None, scal
+    for (axis, bit), piece in zip(rounds, pieces):
+        got = swap(send, axis, bit)
+        for part in piece:
+            *out, mark = grads(scal, act if part[0] == 0 else act_other, xs, gs, part, out, mark, grad_shape, n_group, slots)
+        if axis == "ingroup" and bit == 2:
+            keep, got = keep[0], got[0]
+        keep, *rest = add_halves(keep, got, mark)
+        mark = keep
+        send = rest[0] if rest else None
+    return (keep[0, 0], keep[0, 1], jnp.swapaxes(out[0], 1, 2), jnp.swapaxes(out[1], 1, 2), out[2])
+
+
+def cut(own, n_group, weights):
+    total = own * n_group
+    ends = [total * sum(weights[:k + 1]) // sum(weights) for k in range(len(weights))]
+    pieces, at = [], 0
+    for end in ends:
+        piece = []
+        while at < end:
+            which, first = divmod(at, own)
+            count = min(end - at, own - first)
+            piece.append((which, first, count))
+            at += count
+        pieces.append(piece)
+    return pieces
 
 
 def solution(mesh):

time: 106 us -> 83.7 us (0.79)
  waiting for transfers between devices: 22.4 us -> 9.99 us
  local copies, waits for them, and re-layouts: 8.51 us -> 1.4 us
  other arithmetic: 2.78 us -> 1.01 us
    ppermute x8 -> x12, waiting for transfers between devices: 19.6 us -> 6.36 us  [swap(): return lax.ppermute(x, axis, [(k, k ^ bit) for k in range(n)])]
    unnamed x19 -> x0, local copies, waits for them, and re-layouts: 5.96 us -> none
    pallas_call x1, Pallas kernels: 29.6 us -> 25 us  [shards(): pl.pallas_call(functools.partial(middle_kernel, (n_group, n_ingroup, n_hi...]
    pallas_call x2 -> x9, Pallas kernels: 24.2 us -> 28.1 us  [the longest x4 27.8 us: grads(): pl.pallas_call(functools.partial(grad_kernel, piece, slots, n_group), out...]
    ppermute x3, starting transfers between devices: 7.95 us -> 6.14 us  [shards(): lax.ppermute(message, 'hid', [(k, (k + d) % n_hid) for k in range(n_hid)])]
    ppermute x8 -> x12, starting transfers between devices: 9.54 us -> 11 us  [swap(): return lax.ppermute(x, axis, [(k, k ^ bit) for k in range(n)])]
    add x5 -> x0, other arithmetic: 1.16 us -> none  [the longest x1 1.1 us: shards(): now = part[0] + swap(part[1], 'ingroup', 1)]
    squeeze x3 -> x1, local copies, waits for them, and re-layouts: 1.71 us -> 0.61 us  [shards(): keep[0, 1]]
  transfers between devices with their start and end apart: 11 -> 15, of which waited for: 8 -> 5; matrix products, arithmetic and copies ran while one was open for 1% -> 0% of each run, Pallas kernels for 23% -> 33%
where the time goes in v2:
time: 83.7 us; the launch traced here: 83.5 us
  Pallas kernels  53.1 us (63%)
  starting transfers between devices  17.2 us (21%)
  waiting for transfers between devices  9.99 us (12%)
  local copies, waits for them, and re-layouts  1.4 us (2%)
  other arithmetic  1.01 us (1%)
    pallas_call x4, Pallas kernels, grads(): pl.pallas_call(functools.partial(grad_kernel, piece, slots, n_group), out...  27.8 us
    pallas_call x1, Pallas kernels, shards(): pl.pallas_call(functools.partial(middle_kernel, (n_group, n_ingroup, n_hi...  25 us
    ppermute x12, starting transfers between devices, swap(): return lax.ppermute(x, axis, [(k, k ^ bit) for k in range(n)])  11 us
    ppermute x12, waiting for transfers between devices, swap(): return lax.ppermute(x, axis, [(k, k ^ bit) for k in range(n)])  6.36 us
    ppermute x3, starting transfers between devices, shards(): lax.ppermute(message, 'hid', [(k, (k + d) % n_hid) for k in range(n_hid)])  6.14 us
    ppermute x3, waiting for transfers between devices, shards(): lax.ppermute(message, 'hid', [(k, (k + d) % n_hid) for k in range(n_hid)])  3.62 us
  transfers between devices with their start and end apart: 15, of which 5 were waited for; matrix products, arithmetic and copies ran while one was open for 0% of the time, Pallas kernels for 33%

profile of v2, /device:TPU:0, one launch (start us, length us, event | category | flops | bytes accessed | tf_op | source)
XLA Modules:
  0.0 83.5 jit_solution(17680317756436704161)
XLA Ops:
  0.6 0.8 select_reduce_fusion
  1.5 0.8 constant_dynamic-slice_fusion
  2.3 3.1 %collective-permute-start = (bf16[16,2176]{1,0:T(8,128)(2,1)S(1)}, bf16[16,2176]{1,0:T(8,128)(2,1)S(1)}, u32[]{:S(2)}, u32[]{:S(2)}) collective-permute-start(bf16[16,2176]{1,0:T(8,128)(2,1)S(1)} %get-tuple-element.64), channel_id=1, source_target_pairs={{0,1},{1,2},{2,3},{3,0},{4,5},{5,6},{6,7},{7,4},{8,9},{9,10},{10,1... | collective-permute-start | bytes 208904 | tf_op jit(solution)/shard_map/ppermute | solution.py:310
  5.4 2.1 %collective-permute-start.5 = (bf16[16,2176]{1,0:T(8,128)(2,1)S(1)}, bf16[16,2176]{1,0:T(8,128)(2,1)S(1)}, u32[]{:S(2)}, u32[]{:S(2)}) collective-permute-start(bf16[16,2176]{1,0:T(8,128)(2,1)S(1)} %get-tuple-element.64), channel_id=1, source_target_pairs={{0,3},{1,0},{2,1},{3,2},{4,7},{5,4},{6,5},{7,6},{8,11},{9,8},{10,9... | collective-permute-start | bytes 208904 | tf_op jit(solution)/shard_map/ppermute | solution.py:310
  7.5 0.9 %collective-permute-start.4 = (bf16[16,2176]{1,0:T(8,128)(2,1)S(1)}, bf16[16,2176]{1,0:T(8,128)(2,1)S(1)}, u32[]{:S(2)}, u32[]{:S(2)}) collective-permute-start(bf16[16,2176]{1,0:T(8,128)(2,1)S(1)} %get-tuple-element.64), channel_id=1, source_target_pairs={{0,2},{1,3},{2,0},{3,1},{4,6},{5,7},{6,4},{7,5},{8,10},{9,11},{10,... | collective-permute-start | bytes 208904 | tf_op jit(solution)/shard_map/ppermute | solution.py:310
  8.5 1.4 %collective-permute-done = bf16[16,2176]{1,0:T(8,128)(2,1)S(1)} collective-permute-done((bf16[16,2176]{1,0:T(8,128)(2,1)S(1)}, bf16[16,2176]{1,0:T(8,128)(2,1)S(1)}, u32[]{:S(2)}, u32[]{:S(2)}) %collective-permute-start) | collective-permute-done | bytes 69664 | tf_op jit(solution)/shard_map/ppermute | solution.py:310
  9.9 2.0 %collective-permute-start.2 = (bf16[2,16,2176]{2,1,0:T(8,128)(2,1)S(1)}, bf16[2,16,2176]{2,1,0:T(8,128)(2,1)S(1)}, u32[]{:S(2)}, u32[]{:S(2)}) collective-permute-start(bf16[2,16,2176]{2,1,0:T(8,128)(2,1)S(1)} %pad_maximum_fusion.refs_0_), channel_id=1, source_target_pairs={{0,16},{16,0},{1,17},{17,1},{2,18},{18,2},{3,19},{19,3},{4,20},{20... | collective-permute-start | bytes 417800 | tf_op jit(solution)/shard_map/ppermute | solution.py:280
  11.9 2.2 %collective-permute-done.4 = bf16[16,2176]{1,0:T(8,128)(2,1)S(1)} collective-permute-done((bf16[16,2176]{1,0:T(8,128)(2,1)S(1)}, bf16[16,2176]{1,0:T(8,128)(2,1)S(1)}, u32[]{:S(2)}, u32[]{:S(2)}) %collective-permute-start.4) | collective-permute-done | bytes 69664 | tf_op jit(solution)/shard_map/ppermute | solution.py:310
  14.2 1.6 %collective-permute-start.7 = (bf16[2,16,2176]{2,1,0:T(8,128)(2,1)S(1)}, bf16[2,16,2176]{2,1,0:T(8,128)(2,1)S(1)}, u32[]{:S(2)}, u32[]{:S(2)}) collective-permute-start(bf16[2,16,2176]{2,1,0:T(8,128)(2,1)S(1)} %pad_maximum_fusion.1.refs_4_), channel_id=1, source_target_pairs={{0,16},{16,0},{1,17},{17,1},{2,18},{18,2},{3,19},{19,3},{4,20},{20... | collective-permute-start | bytes 417800 | tf_op jit(solution)/shard_map/ppermute | solution.py:280
  15.7 0.5 collective-permute-start.6
  16.2 3.3 %collective-permute-done.7.refs_6_ = bf16[2,16,2176]{2,1,0:T(8,128)(2,1)S(1)} collective-permute-done((bf16[2,16,2176]{2,1,0:T(8,128)(2,1)S(1)}, bf16[2,16,2176]{2,1,0:T(8,128)(2,1)S(1)}, u32[]{:S(2)}, u32[]{:S(2)}) %collective-permute-start.7) | collective-permute-done | bytes 139296 | tf_op jit(solution)/shard_map/ppermute | solution.py:280
  19.6 1.3 %collective-permute-done.8.refs_7_ = bf16[2,16,2176]{2,1,0:T(8,128)(2,1)S(1)} collective-permute-done((bf16[2,16,2176]{2,1,0:T(8,128)(2,1)S(1)}, bf16[2,16,2176]{2,1,0:T(8,128)(2,1)S(1)}, u32[]{:S(2)}, u32[]{:S(2)}) %collective-permute-start.8) | collective-permute-done | bytes 139296 | tf_op jit(solution)/shard_map/ppermute | solution.py:280
  20.9 25.0 %experts.1 = (bf16[2,8,2,16,512]{4,3,2,1,0:T(8,128)(2,1)S(1)}, bf16[2,8,2,16,512]{4,3,2,1,0:T(8,128)(2,1)S(1)}, bf16[3,128,352]{2,1,0:T(8,128)(2,1)S(1)}, bf16[2...) custom-call(s32[3]{0:T(128)S(1)} %pad_add_fusion.scal.mark_ref, bf16[16,352,2048]{2,1,0:T(8,128)(2,1)} %bitcast.22, ...), custom_call_target="tpu_custom_call" | custom-call | flops 8858370048 | bytes 34603008 | tf_op jit(solution)/shard_map/experts/pallas_call | solution.py:324
  45.9 0.2 collective-permute-start.9
  46.1 1.8 %collective-permute-done.9.got_ref = bf16[2,8,2,16,512]{4,3,2,1,0:T(8,128)(2,1)S(1)} collective-permute-done((bf16[2,8,2,16,512]{4,3,2,1,0:T(8,128)(2,1)S(1)}, bf16[2,8,2,16,512]{4,3,2,1,0:T(8,128)(2,1)S(1)}, u32[]{:S(2)}, u32[]{:S(2)}) %collective-permute-start.9) | collective-permute-done | bytes 524320 | tf_op jit(solution)/shard_map/ppermute | solution.py:280
  48.0 1.4 %collective-permute-start.10 = (bf16[1,8,2,16,512]{4,3,2,1,0:T(8,128)(2,1)S(1)}, bf16[1,8,2,16,512]{4,3,2,1,0:T(8,128)(2,1)S(1)}, u32[]{:S(2)}, u32[]{:S(2)}) collective-permute-start(bf16[1,8,2,16,512]{4,3,2,1,0:T(8,128)(2,1)S(1)} %get-tuple-element.37), channel_id=1, source_target_pairs={{0,8},{4,12},{8,0},{12,4},{1,9},{5,13},{9,1},{13,5},{2,10},{6,14},... | collective-permute-start | bytes 786440 | tf_op jit(solution)/shard_map/ppermute | solution.py:280
  49.5 1.5 %collective-permute-start.13 = (bf16[3,128,352]{2,1,0:T(8,128)(2,1)S(1)}, bf16[3,128,352]{2,1,0:T(8,128)(2,1)S(1)}, u32[]{:S(2)}, u32[]{:S(2)}) collective-permute-start(bf16[3,128,352]{2,1,0:T(8,128)(2,1)S(1)} %get-tuple-element.38.act_ref), channel_id=1, source_target_pairs={{0,16},{16,0},{1,17},{17,1},{2,18},{18,2},{3,19},{19,3},{4,20},{20... | collective-permute-start | bytes 811016 | tf_op jit(solution)/shard_map/ppermute | solution.py:280
  50.9 7.0 %weight_grads.4 = (f32[16,352,1024]{2,1,0:T(8,128)}, f32[16,352,1024]{2,1,0:T(8,128)}, f32[16,352,1024]{2,1,0:T(8,128)}, f32[8,128]{1,0:T(8,128)S(1)}) custom-call(s32[3]{0:T(128)S(1)} %pad_add_fusion.scal.mark_ref, bf16[3,128,352]{2,1,0:T(8,128)(2,1)S(1)} %get-tuple-element.38.act_ref, bf16[2,128,1024]{2,1,0:T(8,128)(2,1)S(1)} %get-tuple-element.39.xs_ref, ...), custom_call_target="tpu_custom_call" | custom-call | flops 138412032 | bytes 17301504 | tf_op jit(solution)/shard_map/weight_grads/pallas_call | solution.py:263
  58.0 0.6 collective-permute-start.11
  58.6 7.0 %weight_grads.5 = (f32[16,352,1024]{2,1,0:T(8,128)}, f32[16,352,1024]{2,1,0:T(8,128)}, f32[16,352,1024]{2,1,0:T(8,128)}, f32[8,128]{1,0:T(8,128)S(1)}) custom-call(s32[3]{0:T(128)S(1)} %pad_add_fusion.scal.mark_ref, bf16[3,128,352]{2,1,0:T(8,128)(2,1)S(1)} %get-tuple-element.38.act_ref, ...), custom_call_target="tpu_custom_call", output_to_operand_aliasing={{0}: (5, {}), {1}: (6, {}), {2}: (7, {})} | custom-call | flops 138412032 | bytes 17301504 | tf_op jit(solution)/shard_map/weight_grads/pallas_call | solution.py:263
  65.7 7.0 %weight_grads.6 = (f32[16,352,1024]{2,1,0:T(8,128)}, f32[16,352,1024]{2,1,0:T(8,128)}, f32[16,352,1024]{2,1,0:T(8,128)}, f32[8,128]{1,0:T(8,128)S(1)}) custom-call(s32[3]{0:T(128)S(1)} %pad_add_fusion.scal.mark_ref, bf16[3,128,352]{2,1,0:T(8,128)(2,1)S(1)} %collective-permute-done.13.act_ref, ...), custom_call_target="tpu_custom_call", output_to_operand_aliasing={{0}: (5, {}), {1}: (6, {}), {2}: (7, {})} | custom-call | flops 138412032 | bytes 17301504 | tf_op jit(solution)/shard_map/weight_grads/pallas_call | solution.py:263
  72.7 3.1 %collective-permute-start.14 = (bf16[1,2,16,512]{3,2,1,0:T(8,128)(2,1)S(1)}, bf16[1,2,16,512]{3,2,1,0:T(8,128)(2,1)S(1)}, u32[]{:S(2)}, u32[]{:S(2)}) collective-permute-start(bf16[1,2,16,512]{3,2,1,0:T(8,128)(2,1)S(1)} %get-tuple-element.55), channel_id=1, source_target_pairs={{0,1},{1,0},{2,3},{3,2},{4,5},{5,4},{6,7},{7,6},{8,9},{9,8},{10,11... | collective-permute-start | bytes 98312 | tf_op jit(solution)/shard_map/ppermute | solution.py:280
  75.9 7.0 %weight_grads.7 = (f32[16,352,1024]{2,1,0:T(8,128)}, f32[16,352,1024]{2,1,0:T(8,128)}, f32[16,352,1024]{2,1,0:T(8,128)}, f32[8,128]{1,0:T(8,128)S(1)}) custom-call(s32[3]{0:T(128)S(1)} %pad_add_fusion.scal.mark_ref, bf16[3,128,352]{2,1,0:T(8,128)(2,1)S(1)} %collective-permute-done.13.act_ref, ...), custom_call_target="tpu_custom_call", output_to_operand_aliasing={{0}: (5, {}), {1}: (6, {}), {2}: (7, {})} | custom-call | flops 138412032 | bytes 17301504 | tf_op jit(solution)/shard_map/weight_grads/pallas_call | solution.py:263
  82.9 0.6 slice_bitcast_fusion
  (25 shorter events, 0.6 us)
Async XLA Ops:
  2.3 7.6 %collective-permute-start = (bf16[16,2176]{1,0:T(8,128)(2,1)S(1)}, bf16[16,2176]{1,0:T(8,128)(2,1)S(1)}, u32[]{:S(2)}, u32[]{:S(2)}) collective-permute-start(bf16[16,2176]{1,0:T(8,128)(2,1)S(1)} %get-tuple-element.64), channel_id=1, source_target_pairs={{0,1},{1,2},{2,3},{3,0},{4,5},{5,6},{6,7},{7,4},{8,9},{9,10},{10,1... | collective-permute-start | bytes 208904 | tf_op jit(solution)/shard_map/ppermute | solution.py:310
  5.4 6.5 %collective-permute-start.5 = (bf16[16,2176]{1,0:T(8,128)(2,1)S(1)}, bf16[16,2176]{1,0:T(8,128)(2,1)S(1)}, u32[]{:S(2)}, u32[]{:S(2)}) collective-permute-start(bf16[16,2176]{1,0:T(8,128)(2,1)S(1)} %get-tuple-element.64), channel_id=1, source_target_pairs={{0,3},{1,0},{2,1},{3,2},{4,7},{5,4},{6,5},{7,6},{8,11},{9,8},{10,9... | collective-permute-start | bytes 208904 | tf_op jit(solution)/shard_map/ppermute | solution.py:310
  7.5 6.6 %collective-permute-start.4 = (bf16[16,2176]{1,0:T(8,128)(2,1)S(1)}, bf16[16,2176]{1,0:T(8,128)(2,1)S(1)}, u32[]{:S(2)}, u32[]{:S(2)}) collective-permute-start(bf16[16,2176]{1,0:T(8,128)(2,1)S(1)} %get-tuple-element.64), channel_id=1, source_target_pairs={{0,2},{1,3},{2,0},{3,1},{4,6},{5,7},{6,4},{7,5},{8,10},{9,11},{10,... | collective-permute-start | bytes 208904 | tf_op jit(solution)/shard_map/ppermute | solution.py:310
  9.9 6.3 %collective-permute-start.2 = (bf16[2,16,2176]{2,1,0:T(8,128)(2,1)S(1)}, bf16[2,16,2176]{2,1,0:T(8,128)(2,1)S(1)}, u32[]{:S(2)}, u32[]{:S(2)}) collective-permute-start(bf16[2,16,2176]{2,1,0:T(8,128)(2,1)S(1)} %pad_maximum_fusion.refs_0_), channel_id=1, source_target_pairs={{0,16},{16,0},{1,17},{17,1},{2,18},{18,2},{3,19},{19,3},{4,20},{20... | collective-permute-start | bytes 417800 | tf_op jit(solution)/shard_map/ppermute | solution.py:280
  14.2 5.4 %collective-permute-start.7 = (bf16[2,16,2176]{2,1,0:T(8,128)(2,1)S(1)}, bf16[2,16,2176]{2,1,0:T(8,128)(2,1)S(1)}, u32[]{:S(2)}, u32[]{:S(2)}) collective-permute-start(bf16[2,16,2176]{2,1,0:T(8,128)(2,1)S(1)} %pad_maximum_fusion.1.refs_4_), channel_id=1, source_target_pairs={{0,16},{16,0},{1,17},{17,1},{2,18},{18,2},{3,19},{19,3},{4,20},{20... | collective-permute-start | bytes 417800 | tf_op jit(solution)/shard_map/ppermute | solution.py:280
  15.7 3.9 %collective-permute-start.1 = (bf16[2,16,2176]{2,1,0:T(8,128)(2,1)S(1)}, bf16[2,16,2176]{2,1,0:T(8,128)(2,1)S(1)}, u32[]{:S(2)}, u32[]{:S(2)}) collective-permute-start(bf16[2,16,2176]{2,1,0:T(8,128)(2,1)S(1)} %pad_maximum_fusion.refs_0_), channel_id=1, source_target_pairs={{0,4},{4,0},{8,12},{12,8},{1,5},{5,1},{9,13},{13,9},{2,6},{6,2},{1... | collective-permute-start | bytes 417800 | tf_op jit(solution)/shard_map/ppermute | solution.py:280
  15.7 3.9 %collective-permute-start.6 = (bf16[2,16,2176]{2,1,0:T(8,128)(2,1)S(1)}, bf16[2,16,2176]{2,1,0:T(8,128)(2,1)S(1)}, u32[]{:S(2)}, u32[]{:S(2)}) collective-permute-start(bf16[2,16,2176]{2,1,0:T(8,128)(2,1)S(1)} %pad_maximum_fusion.1.refs_4_), channel_id=1, source_target_pairs={{0,4},{4,0},{8,12},{12,8},{1,5},{5,1},{9,13},{13,9},{2,6},{6,2},{1... | collective-permute-start | bytes 417800 | tf_op jit(solution)/shard_map/ppermute | solution.py:280
  16.2 3.4 %collective-permute-start.3 = (bf16[2,16,2176]{2,1,0:T(8,128)(2,1)S(1)}, bf16[2,16,2176]{2,1,0:T(8,128)(2,1)S(1)}, u32[]{:S(2)}, u32[]{:S(2)}) collective-permute-start(bf16[2,16,2176]{2,1,0:T(8,128)(2,1)S(1)} %collective-permute-done.2.refs_2_), channel_id=1, source_target_pairs={{0,4},{4,0},{8,12},{12,8},{1,5},{5,1},{9,13},{13,9},{2,6},{6,2},{1... | collective-permute-start | bytes 417800 | tf_op jit(solution)/shard_map/ppermute | solution.py:280
  19.5 1.4 %collective-permute-start.8 = (bf16[2,16,2176]{2,1,0:T(8,128)(2,1)S(1)}, bf16[2,16,2176]{2,1,0:T(8,128)(2,1)S(1)}, u32[]{:S(2)}, u32[]{:S(2)}) collective-permute-start(bf16[2,16,2176]{2,1,0:T(8,128)(2,1)S(1)} %collective-permute-done.7.refs_6_), channel_id=1, source_target_pairs={{0,4},{4,0},{8,12},{12,8},{1,5},{5,1},{9,13},{13,9},{2,6},{6,2},{1... | collective-permute-start | bytes 417800 | tf_op jit(solution)/shard_map/ppermute | solution.py:280
  45.9 2.0 %collective-permute-start.9 = (bf16[2,8,2,16,512]{4,3,2,1,0:T(8,128)(2,1)S(1)}, bf16[2,8,2,16,512]{4,3,2,1,0:T(8,128)(2,1)S(1)}, u32[]{:S(2)}, u32[]{:S(2)}) collective-permute-start(bf16[2,8,2,16,512]{4,3,2,1,0:T(8,128)(2,1)S(1)} %get-tuple-element.35), channel_id=1, source_target_pairs={{0,4},{4,0},{8,12},{12,8},{1,5},{5,1},{9,13},{13,9},{2,6},{6,2},{1... | collective-permute-start | bytes 1572872 | tf_op jit(solution)/shard_map/ppermute | solution.py:280
  48.0 9.9 %collective-permute-start.10 = (bf16[1,8,2,16,512]{4,3,2,1,0:T(8,128)(2,1)S(1)}, bf16[1,8,2,16,512]{4,3,2,1,0:T(8,128)(2,1)S(1)}, u32[]{:S(2)}, u32[]{:S(2)}) collective-permute-start(bf16[1,8,2,16,512]{4,3,2,1,0:T(8,128)(2,1)S(1)} %get-tuple-element.37), channel_id=1, source_target_pairs={{0,8},{4,12},{8,0},{12,4},{1,9},{5,13},{9,1},{13,5},{2,10},{6,14},... | collective-permute-start | bytes 786440 | tf_op jit(solution)/shard_map/ppermute | solution.py:280
  49.5 16.2 %collective-permute-start.13 = (bf16[3,128,352]{2,1,0:T(8,128)(2,1)S(1)}, bf16[3,128,352]{2,1,0:T(8,128)(2,1)S(1)}, u32[]{:S(2)}, u32[]{:S(2)}) collective-permute-start(bf16[3,128,352]{2,1,0:T(8,128)(2,1)S(1)} %get-tuple-element.38.act_ref), channel_id=1, source_target_pairs={{0,16},{16,0},{1,17},{17,1},{2,18},{18,2},{3,19},{19,3},{4,20},{20... | collective-permute-start | bytes 811016 | tf_op jit(solution)/shard_map/ppermute | solution.py:280
  58.0 7.6 %collective-permute-start.11 = (bf16[4,2,16,512]{3,2,1,0:T(8,128)(2,1)S(1)}, bf16[4,2,16,512]{3,2,1,0:T(8,128)(2,1)S(1)}, u32[]{:S(2)}, u32[]{:S(2)}) collective-permute-start(bf16[4,2,16,512]{3,2,1,0:T(8,128)(2,1)S(1)} %get-tuple-element.43), channel_id=1, source_target_pairs={{0,16},{16,0},{1,17},{17,1},{2,18},{18,2},{3,19},{19,3},{4,20},{20... | collective-permute-start | bytes 393224 | tf_op jit(solution)/shard_map/ppermute | solution.py:280
  65.6 7.1 %collective-permute-start.12 = (bf16[2,2,16,512]{3,2,1,0:T(8,128)(2,1)S(1)}, bf16[2,2,16,512]{3,2,1,0:T(8,128)(2,1)S(1)}, u32[]{:S(2)}, u32[]{:S(2)}) collective-permute-start(bf16[2,2,16,512]{3,2,1,0:T(8,128)(2,1)S(1)} %get-tuple-element.49), channel_id=1, source_target_pairs={{0,2},{1,3},{2,0},{3,1},{4,6},{5,7},{6,4},{7,5},{8,10},{9,11},{10,... | collective-permute-start | bytes 196616 | tf_op jit(solution)/shard_map/ppermute | solution.py:280
  72.7 10.1 %collective-permute-start.14 = (bf16[1,2,16,512]{3,2,1,0:T(8,128)(2,1)S(1)}, bf16[1,2,16,512]{3,2,1,0:T(8,128)(2,1)S(1)}, u32[]{:S(2)}, u32[]{:S(2)}) collective-permute-start(bf16[1,2,16,512]{3,2,1,0:T(8,128)(2,1)S(1)} %get-tuple-element.55), channel_id=1, source_target_pairs={{0,1},{1,0},{2,3},{3,2},{4,5},{5,4},{6,7},{7,6},{8,9},{9,8},{10,11... | collective-permute-start | bytes 98312 | tf_op jit(solution)/shard_map/ppermute | solution.py:280

commit v3 on v2

--- a/solution.py
+++ b/solution.py
@@ -100,18 +100,18 @@
     n_group, n_ingroup, n_hid, tok, experts, half, cap = sizes
     message_refs, refs = refs[:2 * len(places)], refs[2 * len(places):]
     keep_ref, send_ref, act_ref, xs_ref, gs_ref = refs[:5]
-    x_scr, g_scr, c_scr, w_scr, pick_scr, wbuf, acc_o, acc_i, sem = refs[5:]
-    ff, width = wbuf.shape[2], wbuf.shape[3]
-    exp_own = wbuf.shape[1]
+    x_scr, g_scr, c_scr, w_scr, pick_scr, wbuf, val_scr, acc_o, acc_i, sem = refs[5:]
+    ff, width = act_ref.shape[2], wbuf.shape[2]
+    exp_own = wbuf.shape[1] // ff
     rows = n_group * n_hid * tok
     wide = width // 2
     g, i, h = scal[0], scal[1], scal[2]
     core = lax.rem(i, 2)
     base = g * exp_own
-    pair = 2
+    pair = 4
 
     def fetch(e, k, ref):
-        return pltpu.make_async_copy(ref.at[base + e], wbuf.at[k, e], sem.at[k, e])
+        return pltpu.make_async_copy(ref.at[base + e], wbuf.at[k, pl.ds(pl.multiple_of(e * ff, ff), ff)], sem.at[k, e])
 
     for e0 in range(0, exp_own, pair):
         for k, ref in enumerate((wg_ref, wu_ref, wd_ref)):
@@ -157,23 +157,23 @@
         gs_ref[which] = jnp.dot(pick, g_scr[:, pl.ds(pl.multiple_of(g * wide, wide), wide)],
                                 preferred_element_type=jnp.float32).astype(jnp.bfloat16)
 
-    acc_o[...] = jnp.zeros_like(acc_o)
-    acc_i[...] = jnp.zeros_like(acc_i)
     nt = (((1,), (1,)), ((), ()))
     lane_f = lax.broadcasted_iota(jnp.int32, (rows, pair * ff), 1)
 
     def step(j, carry):
         e0 = j * pair
-        w, pre = [], []
+        w_at = pl.ds(pl.multiple_of(e0 * ff, pair * ff), pair * ff)
+        pre = []
         for k, (ref, rows_of) in enumerate(((wg_ref, x_scr), (wu_ref, x_scr), (wd_ref, g_scr))):
             for e in range(pair):
                 fetch(e0 + e, k, ref).wait()
-            w.append(wbuf[k, pl.ds(e0, pair)].reshape(pair * ff, width))
-            pre.append(lax.dot_general(rows_of[...], w[k], nt, preferred_element_type=jnp.float32))
+            pre.append(lax.dot_general(rows_of[...], wbuf[k, w_at, :], nt, preferred_element_type=jnp.float32))
         gate, up, back = pre
         at = h * (exp_own * n_group) + base + e0
         col = [jnp.sum(jnp.where(lane == at + e, w_scr[...], 0.0), axis=1, keepdims=True) for e in range(pair)]
-        scale = jnp.where(lane_f < ff, col[0], col[1])
+        scale = col[0]
+        for e in range(1, pair):
+            scale = jnp.where(lane_f < e * ff, scale, col[e])
         sig = jax.nn.sigmoid(gate)
         silu = gate * sig
         d_hid = back * scale
@@ -186,40 +186,41 @@
             for e in range(pair):
                 act_ref[k, pl.ds(pl.multiple_of((e0 + e) * slots, slots), slots), :] = packed[
                     e * slots:(e + 1) * slots, e * ff:(e + 1) * ff]
-        acc_o[...] += jnp.dot(hid, w[2], preferred_element_type=jnp.float32)
-        acc_i[...] += (jnp.dot(d_gate, w[0], preferred_element_type=jnp.float32)
-                       + jnp.dot(d_up, w[1], preferred_element_type=jnp.float32))
+        for k, val in enumerate((d_gate, d_up, hid)):
+            val_scr[k, :, w_at] = val
         return carry
 
     lax.fori_loop(0, exp_own // pair, step, 0)
+    acc_o[...] = jnp.dot(val_scr[2], wbuf[2], preferred_element_type=jnp.float32)
+    acc_i[...] = (jnp.dot(val_scr[0], wbuf[0], preferred_element_type=jnp.float32)
+                  + jnp.dot(val_scr[1], wbuf[1], preferred_element_type=jnp.float32))
     narrow = width // n_ingroup
-    for y in range(n_ingroup // 2):
+    for y in range(2):
         for b in range(n_group * n_hid):
-            rel_y = y ^ (i // 2)
-            rel_b = b ^ (g * n_hid + h)
+            rel = (y ^ (i // 2)) * (n_group * n_hid) + (b ^ (g * n_hid + h))
             at = slice(b * tok, (b + 1) * tok)
             for k, acc in enumerate((acc_o, acc_i)):
                 two = [acc[at, (2 * y + c) * narrow:(2 * y + c + 1) * narrow].astype(jnp.bfloat16) for c in range(2)]
-                keep_ref[rel_y, rel_b, k] = jnp.where(core == 0, two[0], two[1])
-                send_ref[rel_y, rel_b, k] = jnp.where(core == 0, two[1], two[0])
+                keep_ref[rel, k] = jnp.where(core == 0, two[0], two[1])
+                send_ref[rel, k] = jnp.where(core == 0, two[1], two[0])
 
 
 def add_kernel(keep_ref, got_ref, mark_ref, *out_refs):
     del mark_ref
-    size = out_refs[0].shape[0]
+    size = keep_ref.shape[0] // 2
     for k, out in enumerate(out_refs):
-        at = slice(k * size, (k + 1) * size)
+        at = slice(k * size, (k + 1) * size) if size else (0, k)
         out[...] = (keep_ref[at].astype(jnp.float32) + got_ref[at].astype(jnp.float32)).astype(out.dtype)
 
 
 def add_halves(keep, got, mark):
     vmem = pl.BlockSpec(memory_space=pltpu.VMEM)
-    n = 2 if keep.shape[0] > 1 else 1
+    shape = (keep.shape[0] // 2,) + keep.shape[1:] if keep.shape[0] > 1 else keep.shape[2:]
     return pl.pallas_call(
         add_kernel,
-        out_shape=[jax.ShapeDtypeStruct((keep.shape[0] // n,) + keep.shape[1:], keep.dtype)] * n,
+        out_shape=[jax.ShapeDtypeStruct(shape, keep.dtype)] * 2,
         in_specs=[vmem, vmem, pl.BlockSpec(memory_space=pl.ANY)],
-        out_specs=[vmem] * n,
+        out_specs=[vmem] * 2,
         compiler_params=pltpu.CompilerParams(vmem_limit_bytes=4 << 20),
         cost_estimate=pl.CostEstimate(flops=keep.size, bytes_accessed=keep.size * 6, transcendentals=0),
         name="add_halves",
@@ -324,8 +325,8 @@
     keep, send, act, xs, gs = pl.pallas_call(
         functools.partial(middle_kernel, (n_group, n_ingroup, n_hid, tok, experts, half, cap), tuple(places)),
         out_shape=[
-            jax.ShapeDtypeStruct((n_ingroup // 2, n_group * n_hid, 2, tok, narrow), jnp.bfloat16),
-            jax.ShapeDtypeStruct((n_ingroup // 2, n_group * n_hid, 2, tok, narrow), jnp.bfloat16),
+            jax.ShapeDtypeStruct((n_group * n_hid * 2, 2, tok, narrow), jnp.bfloat16),
+            jax.ShapeDtypeStruct((n_group * n_hid * 2, 2, tok, narrow), jnp.bfloat16),
             jax.ShapeDtypeStruct((3, own * slots, ff), jnp.bfloat16),
             jax.ShapeDtypeStruct((n_group, own * slots, half), jnp.bfloat16),
             jax.ShapeDtypeStruct((n_group, own * slots, half), jnp.bfloat16),
@@ -338,12 +339,13 @@
             pltpu.VMEM((2, rows, lanes), jnp.float32),
             pltpu.VMEM((rows, lanes), jnp.float32),
             pltpu.VMEM((own * slots, rows), jnp.bfloat16),
-            pltpu.VMEM((3, own, ff, width), jnp.bfloat16),
+            pltpu.VMEM((3, own * ff, width), jnp.bfloat16),
+            pltpu.VMEM((3, rows, own * ff), jnp.bfloat16),
             pltpu.VMEM((rows, width), jnp.float32),
             pltpu.VMEM((rows, width), jnp.float32),
             pltpu.SemaphoreType.DMA((3, own)),
         ],
-        compiler_params=pltpu.CompilerParams(vmem_limit_bytes=46 << 20),
+        compiler_params=pltpu.CompilerParams(vmem_limit_bytes=48 << 20),
         cost_estimate=pl.CostEstimate(flops=6 * 2 * own * ff * width * rows,
                                       bytes_accessed=3 * own * ff * width * 2, transcendentals=own * ff * rows),
         name="experts",
@@ -355,19 +357,15 @@
     while bit:
         rounds.append(("hid", bit))
         bit //= 2
-    weights = [1] * (len(rounds) - 1)
-    pieces = [[]] + cut(own, n_group, weights)
+    pieces = cut(own, n_group, [0] + [1] * (len(rounds) - 1))
     out, mark = None, scal
     for (axis, bit), piece in zip(rounds, pieces):
         got = swap(send, axis, bit)
         for part in piece:
             *out, mark = grads(scal, act if part[0] == 0 else act_other, xs, gs, part, out, mark, grad_shape, n_group, slots)
-        if axis == "ingroup" and bit == 2:
-            keep, got = keep[0], got[0]
-        keep, *rest = add_halves(keep, got, mark)
+        keep, send = add_halves(keep, got, mark)
         mark = keep
-        send = rest[0] if rest else None
-    return (keep[0, 0], keep[0, 1], jnp.swapaxes(out[0], 1, 2), jnp.swapaxes(out[1], 1, 2), out[2])
+    return (keep, send, jnp.swapaxes(out[0], 1, 2), jnp.swapaxes(out[1], 1, 2), out[2])
 
 
 def cut(own, n_group, weights):

time: 83.7 us -> 80.7 us (0.964)
  Pallas kernels: 53.1 us -> 50.7 us
    pallas_call x1, Pallas kernels: 25 us -> 22 us  [shards(): pl.pallas_call(functools.partial(middle_kernel, (n_group, n_ingroup, n_hi...]
  transfers between devices with their start and end apart: 15 -> 15, of which waited for: 5 -> 5; matrix products, arithmetic and copies ran while one was open for 0% -> 0% of each run, Pallas kernels for 33% -> 35%
where the time goes in v3:
time: 80.7 us; the launch traced here: 80.5 us
  Pallas kernels  50.7 us (63%)
  starting transfers between devices  17.2 us (21%)
  waiting for transfers between devices  9.99 us (12%)
  other arithmetic  1.01 us (1%)
    pallas_call x4, Pallas kernels, grads(): pl.pallas_call(functools.partial(grad_kernel, piece, slots, n_group), out...  27.8 us
    pallas_call x1, Pallas kernels, shards(): pl.pallas_call(functools.partial(middle_kernel, (n_group, n_ingroup, n_hi...  22 us
    ppermute x12, starting transfers between devices, swap(): return lax.ppermute(x, axis, [(k, k ^ bit) for k in range(n)])  11 us
    ppermute x12, waiting for transfers between devices, swap(): return lax.ppermute(x, axis, [(k, k ^ bit) for k in range(n)])  6.36 us
    ppermute x3, starting transfers between devices, shards(): lax.ppermute(message, 'hid', [(k, (k + d) % n_hid) for k in range(n_hid)])  6.14 us
    ppermute x3, waiting for transfers between devices, shards(): lax.ppermute(message, 'hid', [(k, (k + d) % n_hid) for k in range(n_hid)])  3.62 us
  transfers between devices with their start and end apart: 15, of which 5 were waited for; matrix products, arithmetic and copies ran while one was open for 0% of the time, Pallas kernels for 35%

profile of v3, /device:TPU:0, one launch (start us, length us, event | category | flops | bytes accessed | tf_op | source)
XLA Modules:
  0.0 80.5 jit_solution(1916908873049224050)
XLA Ops:
  0.6 0.8 select_reduce_fusion
  1.5 0.8 constant_dynamic-slice_fusion
  2.3 3.1 %collective-permute-start = (bf16[16,2176]{1,0:T(8,128)(2,1)S(1)}, bf16[16,2176]{1,0:T(8,128)(2,1)S(1)}, u32[]{:S(2)}, u32[]{:S(2)}) collective-permute-start(bf16[16,2176]{1,0:T(8,128)(2,1)S(1)} %get-tuple-element.68), channel_id=1, source_target_pairs={{0,1},{1,2},{2,3},{3,0},{4,5},{5,6},{6,7},{7,4},{8,9},{9,10},{10,1... | collective-permute-start | bytes 208904 | tf_op jit(solution)/shard_map/ppermute | solution.py:311
  5.4 2.1 %collective-permute-start.5 = (bf16[16,2176]{1,0:T(8,128)(2,1)S(1)}, bf16[16,2176]{1,0:T(8,128)(2,1)S(1)}, u32[]{:S(2)}, u32[]{:S(2)}) collective-permute-start(bf16[16,2176]{1,0:T(8,128)(2,1)S(1)} %get-tuple-element.68), channel_id=1, source_target_pairs={{0,3},{1,0},{2,1},{3,2},{4,7},{5,4},{6,5},{7,6},{8,11},{9,8},{10,9... | collective-permute-start | bytes 208904 | tf_op jit(solution)/shard_map/ppermute | solution.py:311
  7.5 0.9 %collective-permute-start.4 = (bf16[16,2176]{1,0:T(8,128)(2,1)S(1)}, bf16[16,2176]{1,0:T(8,128)(2,1)S(1)}, u32[]{:S(2)}, u32[]{:S(2)}) collective-permute-start(bf16[16,2176]{1,0:T(8,128)(2,1)S(1)} %get-tuple-element.68), channel_id=1, source_target_pairs={{0,2},{1,3},{2,0},{3,1},{4,6},{5,7},{6,4},{7,5},{8,10},{9,11},{10,... | collective-permute-start | bytes 208904 | tf_op jit(solution)/shard_map/ppermute | solution.py:311
  8.5 1.4 %collective-permute-done = bf16[16,2176]{1,0:T(8,128)(2,1)S(1)} collective-permute-done((bf16[16,2176]{1,0:T(8,128)(2,1)S(1)}, bf16[16,2176]{1,0:T(8,128)(2,1)S(1)}, u32[]{:S(2)}, u32[]{:S(2)}) %collective-permute-start) | collective-permute-done | bytes 69664 | tf_op jit(solution)/shard_map/ppermute | solution.py:311
  9.9 2.0 %collective-permute-start.2 = (bf16[2,16,2176]{2,1,0:T(8,128)(2,1)S(1)}, bf16[2,16,2176]{2,1,0:T(8,128)(2,1)S(1)}, u32[]{:S(2)}, u32[]{:S(2)}) collective-permute-start(bf16[2,16,2176]{2,1,0:T(8,128)(2,1)S(1)} %pad_maximum_fusion.refs_0_), channel_id=1, source_target_pairs={{0,16},{16,0},{1,17},{17,1},{2,18},{18,2},{3,19},{19,3},{4,20},{20... | collective-permute-start | bytes 417800 | tf_op jit(solution)/shard_map/ppermute | solution.py:281
  11.9 2.2 %collective-permute-done.4 = bf16[16,2176]{1,0:T(8,128)(2,1)S(1)} collective-permute-done((bf16[16,2176]{1,0:T(8,128)(2,1)S(1)}, bf16[16,2176]{1,0:T(8,128)(2,1)S(1)}, u32[]{:S(2)}, u32[]{:S(2)}) %collective-permute-start.4) | collective-permute-done | bytes 69664 | tf_op jit(solution)/shard_map/ppermute | solution.py:311
  14.2 1.6 %collective-permute-start.7 = (bf16[2,16,2176]{2,1,0:T(8,128)(2,1)S(1)}, bf16[2,16,2176]{2,1,0:T(8,128)(2,1)S(1)}, u32[]{:S(2)}, u32[]{:S(2)}) collective-permute-start(bf16[2,16,2176]{2,1,0:T(8,128)(2,1)S(1)} %pad_maximum_fusion.1.refs_4_), channel_id=1, source_target_pairs={{0,16},{16,0},{1,17},{17,1},{2,18},{18,2},{3,19},{19,3},{4,20},{20... | collective-permute-start | bytes 417800 | tf_op jit(solution)/shard_map/ppermute | solution.py:281
  15.7 0.5 collective-permute-start.6
  16.2 3.3 %collective-permute-done.7.refs_6_ = bf16[2,16,2176]{2,1,0:T(8,128)(2,1)S(1)} collective-permute-done((bf16[2,16,2176]{2,1,0:T(8,128)(2,1)S(1)}, bf16[2,16,2176]{2,1,0:T(8,128)(2,1)S(1)}, u32[]{:S(2)}, u32[]{:S(2)}) %collective-permute-start.7) | collective-permute-done | bytes 139296 | tf_op jit(solution)/shard_map/ppermute | solution.py:281
  19.6 1.3 %collective-permute-done.8.refs_7_ = bf16[2,16,2176]{2,1,0:T(8,128)(2,1)S(1)} collective-permute-done((bf16[2,16,2176]{2,1,0:T(8,128)(2,1)S(1)}, bf16[2,16,2176]{2,1,0:T(8,128)(2,1)S(1)}, u32[]{:S(2)}, u32[]{:S(2)}) %collective-permute-start.8) | collective-permute-done | bytes 139296 | tf_op jit(solution)/shard_map/ppermute | solution.py:281
  20.9 22.0 %experts.1 = (bf16[16,2,16,512]{3,2,1,0:T(8,128)(2,1)S(1)}, bf16[16,2,16,512]{3,2,1,0:T(8,128)(2,1)S(1)}, bf16[3,128,352]{2,1,0:T(8,128)(2,1)S(1)}, bf16[2,128,1...) custom-call(s32[3]{0:T(128)S(1)} %pad_add_fusion.scal.mark_ref, bf16[16,352,2048]{2,1,0:T(8,128)(2,1)} %bitcast.14, ...), custom_call_target="tpu_custom_call" | custom-call | flops 8858370048 | bytes 34603008 | tf_op jit(solution)/shard_map/experts/pallas_call | solution.py:325
  42.9 0.2 collective-permute-start.9
  43.2 1.8 %collective-permute-done.9.got_ref = bf16[16,2,16,512]{3,2,1,0:T(8,128)(2,1)S(1)} collective-permute-done((bf16[16,2,16,512]{3,2,1,0:T(8,128)(2,1)S(1)}, bf16[16,2,16,512]{3,2,1,0:T(8,128)(2,1)S(1)}, u32[]{:S(2)}, u32[]{:S(2)}) %collective-permute-start.9) | collective-permute-done | bytes 524320 | tf_op jit(solution)/shard_map/ppermute | solution.py:281
  45.0 1.4 %collective-permute-start.10 = (bf16[8,2,16,512]{3,2,1,0:T(8,128)(2,1)S(1)}, bf16[8,2,16,512]{3,2,1,0:T(8,128)(2,1)S(1)}, u32[]{:S(2)}, u32[]{:S(2)}) collective-permute-start(bf16[8,2,16,512]{3,2,1,0:T(8,128)(2,1)S(1)} %get-tuple-element.39), channel_id=1, source_target_pairs={{0,8},{4,12},{8,0},{12,4},{1,9},{5,13},{9,1},{13,5},{2,10},{6,14},... | collective-permute-start | bytes 786440 | tf_op jit(solution)/shard_map/ppermute | solution.py:281
  46.5 1.5 %collective-permute-start.13 = (bf16[3,128,352]{2,1,0:T(8,128)(2,1)S(1)}, bf16[3,128,352]{2,1,0:T(8,128)(2,1)S(1)}, u32[]{:S(2)}, u32[]{:S(2)}) collective-permute-start(bf16[3,128,352]{2,1,0:T(8,128)(2,1)S(1)} %get-tuple-element.40.act_ref), channel_id=1, source_target_pairs={{0,16},{16,0},{1,17},{17,1},{2,18},{18,2},{3,19},{19,3},{4,20},{20... | collective-permute-start | bytes 811016 | tf_op jit(solution)/shard_map/ppermute | solution.py:281
  48.0 7.0 %weight_grads.4 = (f32[16,352,1024]{2,1,0:T(8,128)}, f32[16,352,1024]{2,1,0:T(8,128)}, f32[16,352,1024]{2,1,0:T(8,128)}, f32[8,128]{1,0:T(8,128)S(1)}) custom-call(s32[3]{0:T(128)S(1)} %pad_add_fusion.scal.mark_ref, bf16[3,128,352]{2,1,0:T(8,128)(2,1)S(1)} %get-tuple-element.40.act_ref, bf16[2,128,1024]{2,1,0:T(8,128)(2,1)S(1)} %get-tuple-element.41.xs_ref, ...), custom_call_target="tpu_custom_call" | custom-call | flops 138412032 | bytes 17301504 | tf_op jit(solution)/shard_map/weight_grads/pallas_call | solution.py:264
  55.0 0.6 collective-permute-start.11
  55.6 7.0 %weight_grads.5 = (f32[16,352,1024]{2,1,0:T(8,128)}, f32[16,352,1024]{2,1,0:T(8,128)}, f32[16,352,1024]{2,1,0:T(8,128)}, f32[8,128]{1,0:T(8,128)S(1)}) custom-call(s32[3]{0:T(128)S(1)} %pad_add_fusion.scal.mark_ref, bf16[3,128,352]{2,1,0:T(8,128)(2,1)S(1)} %get-tuple-element.40.act_ref, ...), custom_call_target="tpu_custom_call", output_to_operand_aliasing={{0}: (5, {}), {1}: (6, {}), {2}: (7, {})} | custom-call | flops 138412032 | bytes 17301504 | tf_op jit(solution)/shard_map/weight_grads/pallas_call | solution.py:264
  62.7 7.0 %weight_grads.6 = (f32[16,352,1024]{2,1,0:T(8,128)}, f32[16,352,1024]{2,1,0:T(8,128)}, f32[16,352,1024]{2,1,0:T(8,128)}, f32[8,128]{1,0:T(8,128)S(1)}) custom-call(s32[3]{0:T(128)S(1)} %pad_add_fusion.scal.mark_ref, bf16[3,128,352]{2,1,0:T(8,128)(2,1)S(1)} %collective-permute-done.13.act_ref, ...), custom_call_target="tpu_custom_call", output_to_operand_aliasing={{0}: (5, {}), {1}: (6, {}), {2}: (7, {})} | custom-call | flops 138412032 | bytes 17301504 | tf_op jit(solution)/shard_map/weight_grads/pallas_call | solution.py:264
  69.7 3.2 %collective-permute-start.14 = (bf16[1,2,16,512]{3,2,1,0:T(8,128)(2,1)S(1)}, bf16[1,2,16,512]{3,2,1,0:T(8,128)(2,1)S(1)}, u32[]{:S(2)}, u32[]{:S(2)}) collective-permute-start(bf16[1,2,16,512]{3,2,1,0:T(8,128)(2,1)S(1)} %get-tuple-element.57), channel_id=1, source_target_pairs={{0,1},{1,0},{2,3},{3,2},{4,5},{5,4},{6,7},{7,6},{8,9},{9,8},{10,11... | collective-permute-start | bytes 98312 | tf_op jit(solution)/shard_map/ppermute | solution.py:281
  72.9 7.0 %weight_grads.7 = (f32[16,352,1024]{2,1,0:T(8,128)}, f32[16,352,1024]{2,1,0:T(8,128)}, f32[16,352,1024]{2,1,0:T(8,128)}, f32[8,128]{1,0:T(8,128)S(1)}) custom-call(s32[3]{0:T(128)S(1)} %pad_add_fusion.scal.mark_ref, bf16[3,128,352]{2,1,0:T(8,128)(2,1)S(1)} %collective-permute-done.13.act_ref, ...), custom_call_target="tpu_custom_call", output_to_operand_aliasing={{0}: (5, {}), {1}: (6, {}), {2}: (7, {})} | custom-call | flops 138412032 | bytes 17301504 | tf_op jit(solution)/shard_map/weight_grads/pallas_call | solution.py:264
  79.9 0.6 add_halves.9
  (24 shorter events, 0.6 us)
Async XLA Ops:
  2.3 7.6 %collective-permute-start = (bf16[16,2176]{1,0:T(8,128)(2,1)S(1)}, bf16[16,2176]{1,0:T(8,128)(2,1)S(1)}, u32[]{:S(2)}, u32[]{:S(2)}) collective-permute-start(bf16[16,2176]{1,0:T(8,128)(2,1)S(1)} %get-tuple-element.68), channel_id=1, source_target_pairs={{0,1},{1,2},{2,3},{3,0},{4,5},{5,6},{6,7},{7,4},{8,9},{9,10},{10,1... | collective-permute-start | bytes 208904 | tf_op jit(solution)/shard_map/ppermute | solution.py:311
  5.4 6.5 %collective-permute-start.5 = (bf16[16,2176]{1,0:T(8,128)(2,1)S(1)}, bf16[16,2176]{1,0:T(8,128)(2,1)S(1)}, u32[]{:S(2)}, u32[]{:S(2)}) collective-permute-start(bf16[16,2176]{1,0:T(8,128)(2,1)S(1)} %get-tuple-element.68), channel_id=1, source_target_pairs={{0,3},{1,0},{2,1},{3,2},{4,7},{5,4},{6,5},{7,6},{8,11},{9,8},{10,9... | collective-permute-start | bytes 208904 | tf_op jit(solution)/shard_map/ppermute | solution.py:311
  7.5 6.6 %collective-permute-start.4 = (bf16[16,2176]{1,0:T(8,128)(2,1)S(1)}, bf16[16,2176]{1,0:T(8,128)(2,1)S(1)}, u32[]{:S(2)}, u32[]{:S(2)}) collective-permute-start(bf16[16,2176]{1,0:T(8,128)(2,1)S(1)} %get-tuple-element.68), channel_id=1, source_target_pairs={{0,2},{1,3},{2,0},{3,1},{4,6},{5,7},{6,4},{7,5},{8,10},{9,11},{10,... | collective-permute-start | bytes 208904 | tf_op jit(solution)/shard_map/ppermute | solution.py:311
  9.9 6.3 %collective-permute-start.2 = (bf16[2,16,2176]{2,1,0:T(8,128)(2,1)S(1)}, bf16[2,16,2176]{2,1,0:T(8,128)(2,1)S(1)}, u32[]{:S(2)}, u32[]{:S(2)}) collective-permute-start(bf16[2,16,2176]{2,1,0:T(8,128)(2,1)S(1)} %pad_maximum_fusion.refs_0_), channel_id=1, source_target_pairs={{0,16},{16,0},{1,17},{17,1},{2,18},{18,2},{3,19},{19,3},{4,20},{20... | collective-permute-start | bytes 417800 | tf_op jit(solution)/shard_map/ppermute | solution.py:281
  14.2 5.4 %collective-permute-start.7 = (bf16[2,16,2176]{2,1,0:T(8,128)(2,1)S(1)}, bf16[2,16,2176]{2,1,0:T(8,128)(2,1)S(1)}, u32[]{:S(2)}, u32[]{:S(2)}) collective-permute-start(bf16[2,16,2176]{2,1,0:T(8,128)(2,1)S(1)} %pad_maximum_fusion.1.refs_4_), channel_id=1, source_target_pairs={{0,16},{16,0},{1,17},{17,1},{2,18},{18,2},{3,19},{19,3},{4,20},{20... | collective-permute-start | bytes 417800 | tf_op jit(solution)/shard_map/ppermute | solution.py:281
  15.7 3.9 %collective-permute-start.1 = (bf16[2,16,2176]{2,1,0:T(8,128)(2,1)S(1)}, bf16[2,16,2176]{2,1,0:T(8,128)(2,1)S(1)}, u32[]{:S(2)}, u32[]{:S(2)}) collective-permute-start(bf16[2,16,2176]{2,1,0:T(8,128)(2,1)S(1)} %pad_maximum_fusion.refs_0_), channel_id=1, source_target_pairs={{0,4},{4,0},{8,12},{12,8},{1,5},{5,1},{9,13},{13,9},{2,6},{6,2},{1... | collective-permute-start | bytes 417800 | tf_op jit(solution)/shard_map/ppermute | solution.py:281
  15.7 3.9 %collective-permute-start.6 = (bf16[2,16,2176]{2,1,0:T(8,128)(2,1)S(1)}, bf16[2,16,2176]{2,1,0:T(8,128)(2,1)S(1)}, u32[]{:S(2)}, u32[]{:S(2)}) collective-permute-start(bf16[2,16,2176]{2,1,0:T(8,128)(2,1)S(1)} %pad_maximum_fusion.1.refs_4_), channel_id=1, source_target_pairs={{0,4},{4,0},{8,12},{12,8},{1,5},{5,1},{9,13},{13,9},{2,6},{6,2},{1... | collective-permute-start | bytes 417800 | tf_op jit(solution)/shard_map/ppermute | solution.py:281
  16.2 3.4 %collective-permute-start.3 = (bf16[2,16,2176]{2,1,0:T(8,128)(2,1)S(1)}, bf16[2,16,2176]{2,1,0:T(8,128)(2,1)S(1)}, u32[]{:S(2)}, u32[]{:S(2)}) collective-permute-start(bf16[2,16,2176]{2,1,0:T(8,128)(2,1)S(1)} %collective-permute-done.2.refs_2_), channel_id=1, source_target_pairs={{0,4},{4,0},{8,12},{12,8},{1,5},{5,1},{9,13},{13,9},{2,6},{6,2},{1... | collective-permute-start | bytes 417800 | tf_op jit(solution)/shard_map/ppermute | solution.py:281
  19.5 1.4 %collective-permute-start.8 = (bf16[2,16,2176]{2,1,0:T(8,128)(2,1)S(1)}, bf16[2,16,2176]{2,1,0:T(8,128)(2,1)S(1)}, u32[]{:S(2)}, u32[]{:S(2)}) collective-permute-start(bf16[2,16,2176]{2,1,0:T(8,128)(2,1)S(1)} %collective-permute-done.7.refs_6_), channel_id=1, source_target_pairs={{0,4},{4,0},{8,12},{12,8},{1,5},{5,1},{9,13},{13,9},{2,6},{6,2},{1... | collective-permute-start | bytes 417800 | tf_op jit(solution)/shard_map/ppermute | solution.py:281
  42.9 2.0 %collective-permute-start.9 = (bf16[16,2,16,512]{3,2,1,0:T(8,128)(2,1)S(1)}, bf16[16,2,16,512]{3,2,1,0:T(8,128)(2,1)S(1)}, u32[]{:S(2)}, u32[]{:S(2)}) collective-permute-start(bf16[16,2,16,512]{3,2,1,0:T(8,128)(2,1)S(1)} %get-tuple-element.37), channel_id=1, source_target_pairs={{0,4},{4,0},{8,12},{12,8},{1,5},{5,1},{9,13},{13,9},{2,6},{6,2},{1... | collective-permute-start | bytes 1572872 | tf_op jit(solution)/shard_map/ppermute | solution.py:281
  45.0 9.9 %collective-permute-start.10 = (bf16[8,2,16,512]{3,2,1,0:T(8,128)(2,1)S(1)}, bf16[8,2,16,512]{3,2,1,0:T(8,128)(2,1)S(1)}, u32[]{:S(2)}, u32[]{:S(2)}) collective-permute-start(bf16[8,2,16,512]{3,2,1,0:T(8,128)(2,1)S(1)} %get-tuple-element.39), channel_id=1, source_target_pairs={{0,8},{4,12},{8,0},{12,4},{1,9},{5,13},{9,1},{13,5},{2,10},{6,14},... | collective-permute-start | bytes 786440 | tf_op jit(solution)/shard_map/ppermute | solution.py:281
  46.5 16.2 %collective-permute-start.13 = (bf16[3,128,352]{2,1,0:T(8,128)(2,1)S(1)}, bf16[3,128,352]{2,1,0:T(8,128)(2,1)S(1)}, u32[]{:S(2)}, u32[]{:S(2)}) collective-permute-start(bf16[3,128,352]{2,1,0:T(8,128)(2,1)S(1)} %get-tuple-element.40.act_ref), channel_id=1, source_target_pairs={{0,16},{16,0},{1,17},{17,1},{2,18},{18,2},{3,19},{19,3},{4,20},{20... | collective-permute-start | bytes 811016 | tf_op jit(solution)/shard_map/ppermute | solution.py:281
  55.0 7.6 %collective-permute-start.11 = (bf16[4,2,16,512]{3,2,1,0:T(8,128)(2,1)S(1)}, bf16[4,2,16,512]{3,2,1,0:T(8,128)(2,1)S(1)}, u32[]{:S(2)}, u32[]{:S(2)}) collective-permute-start(bf16[4,2,16,512]{3,2,1,0:T(8,128)(2,1)S(1)} %get-tuple-element.45), channel_id=1, source_target_pairs={{0,16},{16,0},{1,17},{17,1},{2,18},{18,2},{3,19},{19,3},{4,20},{20... | collective-permute-start | bytes 393224 | tf_op jit(solution)/shard_map/ppermute | solution.py:281
  62.6 7.1 %collective-permute-start.12 = (bf16[2,2,16,512]{3,2,1,0:T(8,128)(2,1)S(1)}, bf16[2,2,16,512]{3,2,1,0:T(8,128)(2,1)S(1)}, u32[]{:S(2)}, u32[]{:S(2)}) collective-permute-start(bf16[2,2,16,512]{3,2,1,0:T(8,128)(2,1)S(1)} %get-tuple-element.51), channel_id=1, source_target_pairs={{0,2},{1,3},{2,0},{3,1},{4,6},{5,7},{6,4},{7,5},{8,10},{9,11},{10,... | collective-permute-start | bytes 196616 | tf_op jit(solution)/shard_map/ppermute | solution.py:281
  69.7 10.1 %collective-permute-start.14 = (bf16[1,2,16,512]{3,2,1,0:T(8,128)(2,1)S(1)}, bf16[1,2,16,512]{3,2,1,0:T(8,128)(2,1)S(1)}, u32[]{:S(2)}, u32[]{:S(2)}) collective-permute-start(bf16[1,2,16,512]{3,2,1,0:T(8,128)(2,1)S(1)} %get-tuple-element.57), channel_id=1, source_target_pairs={{0,1},{1,0},{2,3},{3,2},{4,5},{5,4},{6,7},{7,6},{8,9},{9,8},{10,11... | collective-permute-start | bytes 98312 | tf_op jit(solution)/shard_map/ppermute | solution.py:281
